TPU v7x, 512 devices: a whole 4x4x16 slice. The times are simulated.
512 devices in a mesh: row: 32 (over y, x, core), col: 16 (over z).
Axes of the slice: x: 4, y: 4, z: 16, core: 2. Of those that a mesh axis runs over, the one named last changes fastest.
Arguments:
- kernel: bfloat16 [16, 32, 16, 16, 512], P(None, 'row', None, 'col'), as said below
Outputs:
- factor: float32 [16, 32, 16, 16, 512], P(None, 'row', None, 'col')
Inputs may be any that keep to these rules, and one draw needn't show every extreme that they name: kernel holds a symmetric positive definite matrix.
All inputs are finite; a program needn't handle non-finite values.
Results may differ from a plain program's by a relative error of at most 0.0046.
Values may be sent and summed in bfloat16 or wider, within the bound.
A program may use at most 64 MiB of HBM per device.

v0:
```python
import jax
import jax.numpy as jnp
from jax import lax
from jax.experimental import pallas as pl
from jax.experimental.pallas import tpu as pltpu
from jax.sharding import PartitionSpec as P

P_SIZE = 512
NT = 16


def bf16_gram(left_side, right_side):
    return lax.dot_general(
        left_side.astype(jnp.bfloat16),
        right_side.astype(jnp.bfloat16),
        (((1,), (1,)), ((), ())),
        preferred_element_type=jnp.float32,
    )


BLOCK = 128
EXACT = lax.Precision.HIGHEST


def exact_dot(left_side, right_side):
    return lax.dot_general(
        left_side, right_side, (((1,), (1,)), ((), ())),
        precision=EXACT, preferred_element_type=jnp.float32,
    )


def factor_kernel(sym_ref, low_ref, inv_ref, work_ref, diag_ref, dinv_ref):
    size = sym_ref.shape[0]
    blocks = size // BLOCK
    work_ref[...] = sym_ref[...]
    low_ref[...] = jnp.zeros_like(low_ref)
    inv_ref[...] = jnp.zeros_like(inv_ref)
    rows = lax.broadcasted_iota(jnp.int32, (BLOCK, BLOCK), 0)
    lanes = lax.broadcasted_iota(jnp.int32, (BLOCK, BLOCK), 1)
    col_ids = lax.broadcasted_iota(jnp.int32, (BLOCK, 1), 0)
    row_ids = lax.broadcasted_iota(jnp.int32, (1, BLOCK), 1)
    eye = jnp.where(rows == lanes, 1.0, 0.0).astype(jnp.float32)
    for k in range(blocks):
        here = pl.ds(k * BLOCK, BLOCK)
        diag_ref[...] = jnp.zeros((BLOCK, BLOCK), jnp.float32)
        dinv_ref[...] = eye

        def step(j, block):
            col = jnp.sum(jnp.where(lanes == j, block, 0.0), axis=1, keepdims=True)
            row = jnp.sum(jnp.where(rows == j, block, 0.0), axis=0, keepdims=True)
            pivot = jnp.sum(jnp.where(col_ids == j, col, 0.0), axis=0, keepdims=True)
            root = jnp.sqrt(pivot)
            scale = 1.0 / root
            c_col = jnp.where(col_ids > j, col * scale, jnp.where(col_ids == j, root, 0.0))
            c_row = jnp.where(row_ids > j, row * scale, jnp.where(row_ids == j, root, 0.0))
            diag_ref[...] = jnp.where(lanes == j, c_col, diag_ref[...])
            inverse = dinv_ref[...]
            inv_row = jnp.sum(jnp.where(rows == j, inverse, 0.0), axis=0, keepdims=True)
            shift = jnp.where(col_ids == j, (root - 1.0) * scale, c_col * scale)
            dinv_ref[...] = inverse - shift * inv_row
            return block - c_col * c_row

        lax.fori_loop(0, BLOCK, step, work_ref[here, here])
        low_ref[here, here] = diag_ref[...]
        inv_ref[here, here] = dinv_ref[...]
        if k + 1 < blocks:
            rest = pl.ds((k + 1) * BLOCK, size - (k + 1) * BLOCK)
            panel = exact_dot(work_ref[rest, here], dinv_ref[...])
            low_ref[rest, here] = panel
            work_ref[rest, rest] = work_ref[rest, rest] - exact_dot(panel, panel)
    for i in range(1, blocks):
        at_i = pl.ds(i * BLOCK, BLOCK)
        for k in range(i):
            at_k = pl.ds(k * BLOCK, BLOCK)
            total = jnp.zeros((BLOCK, BLOCK), jnp.float32)
            for m in range(k, i):
                at_m = pl.ds(m * BLOCK, BLOCK)
                total = total + jnp.dot(
                    low_ref[at_i, at_m], inv_ref[at_m, at_k],
                    precision=EXACT, preferred_element_type=jnp.float32,
                )
            inv_ref[at_i, at_k] = -jnp.dot(
                inv_ref[at_i, at_i], total,
                precision=EXACT, preferred_element_type=jnp.float32,
            )


def factor_and_inverse(sym):
    size = sym.shape[0]
    return pl.pallas_call(
        factor_kernel,
        out_shape=(
            jax.ShapeDtypeStruct((size, size), jnp.float32),
            jax.ShapeDtypeStruct((size, size), jnp.float32),
        ),
        in_specs=[pl.BlockSpec(memory_space=pltpu.VMEM)],
        out_specs=(
            pl.BlockSpec(memory_space=pltpu.VMEM),
            pl.BlockSpec(memory_space=pltpu.VMEM),
        ),
        scratch_shapes=[
            pltpu.VMEM((size, size), jnp.float32),
            pltpu.VMEM((BLOCK, BLOCK), jnp.float32),
            pltpu.VMEM((BLOCK, BLOCK), jnp.float32),
        ],
    )(sym)


def per_device(kernel):
    row_count = lax.axis_size("row")
    col_count = lax.axis_size("col")
    tile_rows = P_SIZE // row_count
    tile_cols = P_SIZE // col_count
    row_index = lax.axis_index("row")
    column_index = lax.axis_index("col")
    tiles = kernel.reshape(NT, NT, tile_rows, tile_cols)
    local = tiles.transpose(0, 2, 1, 3).reshape(NT * tile_rows, NT * tile_cols)

    with jax.named_scope("gather_inputs"):
        band = lax.all_gather(local[:, : 2 * tile_cols], "col", axis=0)
        band = band.reshape(col_count, NT * tile_rows, 2, tile_cols)
        band = band.transpose(1, 2, 0, 3).reshape(NT * tile_rows, 2 * P_SIZE)
        own_rows = band[tile_rows:].astype(jnp.float32)
        top = jnp.concatenate([band[: 2 * tile_rows], local[: 2 * tile_rows, 2 * tile_cols :]], axis=1)
        top = lax.all_gather(top, "row", axis=0)
        top = top.reshape(row_count, 2, tile_rows, top.shape[-1]).transpose(1, 0, 2, 3)
        top = top.reshape(2 * P_SIZE, top.shape[-1]).astype(jnp.float32)
        corners = jnp.stack(
            [top[:P_SIZE, :P_SIZE], top[P_SIZE:, :P_SIZE], top[P_SIZE : 2 * P_SIZE, P_SIZE : 2 * P_SIZE]]
        )
        own_second = lax.dynamic_slice_in_dim(top, P_SIZE + column_index * tile_cols, tile_cols, 1)
        col_rows = jnp.concatenate([own_second, top[:, 2 * P_SIZE :]], axis=1).T

    with jax.named_scope("first_panel"):
        first_factor, first_inverse = factor_and_inverse(0.5 * (corners[0] + corners[0].T))
        own_count = (NT - 1) * tile_rows
        col_total = (NT - 1) * tile_cols
        stacked = jnp.concatenate(
            [corners[1], own_rows[:, :P_SIZE], col_rows[:, :P_SIZE]], axis=0
        )
        solved = exact_dot(stacked, first_inverse)
        next_rows = solved[:P_SIZE].astype(jnp.bfloat16)
        first_own = solved[P_SIZE : P_SIZE + own_count]
        first_col = solved[P_SIZE + own_count :]

    with jax.named_scope("second_panel"):
        second_corner = corners[2] - bf16_gram(next_rows, next_rows)
        second_factor, second_inverse = factor_and_inverse(0.5 * (second_corner + second_corner.T))
        own_below = own_rows[tile_rows:, P_SIZE:] - bf16_gram(first_own[tile_rows:], next_rows)
        col_below = col_rows[tile_cols:, P_SIZE:] - bf16_gram(first_col[tile_cols:], next_rows)
        solved = exact_dot(jnp.concatenate([own_below, col_below], axis=0), second_inverse)
        second_own = solved[: own_count - tile_rows]
        second_col = solved[own_count - tile_rows :]

    with jax.named_scope("trailing_update"):
        trailing = local[2 * tile_rows :, 2 * tile_cols :]
        trailing = trailing.astype(jnp.float32) - bf16_gram(
            first_own[tile_rows:], first_col[tile_cols:]
        )
        trailing = trailing - bf16_gram(second_own, second_col)

    with jax.named_scope("assemble"):
        start_row = row_index * tile_rows
        start_col = column_index * tile_cols
        first_corner = lax.dynamic_slice(first_factor, (start_row, start_col), (tile_rows, tile_cols))
        second_tile = lax.dynamic_slice(second_factor, (start_row, start_col), (tile_rows, tile_cols))
        first_cols = lax.dynamic_slice_in_dim(first_own, start_col, tile_cols, 1)
        second_cols = lax.dynamic_slice_in_dim(second_own, start_col, tile_cols, 1)
        result = jnp.zeros((NT * tile_rows, NT * tile_cols), jnp.float32)
        result = result.at[:tile_rows, :tile_cols].set(first_corner)
        result = result.at[tile_rows:, :tile_cols].set(first_cols)
        result = result.at[tile_rows : 2 * tile_rows, tile_cols : 2 * tile_cols].set(second_tile)
        result = result.at[2 * tile_rows :, tile_cols : 2 * tile_cols].set(second_cols)
        result = result.at[2 * tile_rows :, 2 * tile_cols :].set(trailing)
        result = result.reshape(NT, tile_rows, NT, tile_cols).transpose(0, 2, 1, 3)
    return result.reshape(NT, 1, NT, 1, tile_rows * tile_cols)


def solution(mesh):
    placed = (P(None, "row", None, "col", None),)
    return jax.shard_map(
        per_device,
        mesh=mesh,
        in_specs=placed,
        out_specs=P(None, "row", None, "col", None),
        check_vma=False,
    )
```

profile of v0, /device:TPU:1, one launch (start us, length us, event | category | flops | bytes accessed | tf_op | source)
XLA Modules:
  0.0 329.5 jit_solution(4842768104188265589)
XLA Ops:
  6.5 1.7 reshape.175
  9.6 35.4 %all-gather = bf16[4096,64]{1,0:T(8,128)(2,1)S(1)} all-gather(bf16[256,64]{1,0:T(8,128)(2,1)S(1)} %slice.200), channel_id=2, replica_groups=mesh['row'=32,'col'=16] {'col'}, dimensions={0}, use_global_device_ids=true | all-gather | bytes 557056 | tf_op jit(solution)/shard_map/gather_inputs/all_gather | solution.py:120
  50.1 60.9 %all-gather.4.cloned.1.call-done = bf16[1024,1472]{1,0:T(8,128)(2,1)} async-done(((bf16[32,1472]{1,0:T(8,128)(2,1)}), bf16[1024,1472]{1,0:T(8,128)(2,1)}) %all-gather.4.cloned.1.call-update) | async-done | bytes 3014672 | tf_op jit(solution)/shard_map/gather_inputs/all_gather | solution.py:125
  111.0 2.8 convert_bitcast_fusion
  114.8 1.3 slice.203
  116.1 1.6 copy-done
  118.0 2.0 copy.42
  120.0 1.6 maximum_bitcast_fusion
  122.6 1.6 copy.39
  124.2 3.8 %fusion.23 = (f32[512,512]{1,0:T(8,128)}, f32[512,512]{1,0:T(8,128)}, f32[512,512]{1,0:T(8,128)}) fusion(f32[1024,1472]{1,0:T(8,128)} %bitcast.42, f32[512,512]{0,1:T(8,128)S(1)} %copy.39), kind=kLoop, calls=%fused_computation.39 | loop fusion | flops 524288 | bytes 7340032 | tf_op jit(solution)/shard_map/gather_inputs/slice | solution.py:129
  128.0 79.1 %first_panel.1 = (f32[512,512]{1,0:T(8,128)}, f32[512,512]{1,0:T(8,128)}) custom-call(f32[512,512]{1,0:T(8,128)} %get-tuple-element.74.sym_ref), custom_call_target="tpu_custom_call" | custom-call | tf_op jit(solution)/shard_map/first_panel/pallas_call | solution.py:90
  207.0 7.6 %fusion.24 = (bf16[1232,512]{1,0:T(8,128)(2,1)S(1)}, f32[1232,512]{1,0:T(8,128)}) fusion(f32[512,512]{1,0:T(8,128)} %get-tuple-element.70, f32[480,512]{1,0:T(8,128)} %slice.208, f32[240,512]{1,0:T(8,128)} %copy.40, f32[512,512]{1,0:T(8,128)} %get-tuple-element.75), kind=kOutput, calls=%fused_computation.40 | convolution fusion | flops 3877429248 | bytes 7356416 | tf_op jit(solution)/shard_map/first_panel/dot_general | solution.py:26
  214.7 1.4 convolution_subtract_fusion.1
  217.3 1.3 copy.43
  218.6 1.7 convolution_subtract_fusion
  220.3 1.3 copy.35
  221.6 2.5 fusion.10.sym_ref
  224.1 79.4 %second_panel.1 = (f32[512,512]{1,0:T(8,128)}, f32[512,512]{1,0:T(8,128)}) custom-call(f32[512,512]{1,0:T(8,128)} %fusion.10.sym_ref), custom_call_target="tpu_custom_call" | custom-call | tf_op jit(solution)/shard_map/second_panel/pallas_call | solution.py:90
  304.7 2.4 fusion.6
  310.4 1.7 scatter.19
  313.1 2.1 scatter.21
  315.2 1.8 scatter.24
  317.6 2.0 copy.37
  319.6 3.1 reshape.179
  (44 shorter events, 15.8 us)
Async XLA Ops:
  6.5 104.4 %all-gather.4.cloned.1.call-start = ((), (), s32[]{:S(2)}) async-start(), calls=%async_computation | async-start | bytes 3244032 | tf_op jit(solution)/shard_map/gather_inputs/all_gather | solution.py:125
  114.6 3.1 copy-start
  216.1 1.2 copy-start.1
  221.6 81.9 %copy-start.3 = (f32[224,512]{1,0:T(8,128)S(1)}, f32[224,512]{1,0:T(8,128)}, u32[]{:S(2)}) copy-start(f32[224,512]{1,0:T(8,128)} %copy.44) | copy-start | bytes 1376260
  224.1 79.7 %copy-start.2 = (f32[448,512]{1,0:T(8,128)S(1)}, f32[448,512]{1,0:T(8,128)}, u32[]{:S(2)}) copy-start(f32[448,512]{1,0:T(8,128)} %convolution_subtract_fusion.1) | copy-start | bytes 2752516
  303.5 1.2 copy-start.4
Sparse Core Ops, SparseCore 0:
  47.1 63.7 all-gather.3
where the time goes:
time: 330 us
  Pallas kernels  158 us (48%)
  waiting for transfers between devices  60.9 us (18%)
  local copies, waits for them, and re-layouts  35.5 us (11%)
  blocking collectives  35.4 us (11%)
  matrix products  14 us (4%)
  between operations  13.7 us (4%)
  other arithmetic  11.5 us (3%)
    pallas_call x2, Pallas kernels, factor_and_inverse(): pl.pallas_call(factor_kernel, out_shape=(jax.ShapeDtypeStruct((size, size...  158 us
    all_gather x1, waiting for transfers between devices, per_device(): top = lax.all_gather(top, 'row', axis=0)  60.9 us
    all_gather x1, blocking collectives, per_device(): band = lax.all_gather(local[:, :2 * tile_cols], 'col', axis=0)  35.4 us
    unnamed x17, local copies, waits for them, and re-layouts  10.4 us
    dot_general x2, matrix products, exact_dot(): lax.dot_general(left_side, right_side, (((1,), (1,)), ((), ())), precisio...  9.99 us
  transfers between devices with their start and end apart: 1, of which 1 were waited for; matrix products, arithmetic and copies ran while one was open for 1% of the time, Pallas kernels for 0%

commit v1 on v0

--- a/solution.py
+++ b/solution.py
@@ -116,27 +116,27 @@
     tiles = kernel.reshape(NT, NT, tile_rows, tile_cols)
     local = tiles.transpose(0, 2, 1, 3).reshape(NT * tile_rows, NT * tile_cols)
 
+    with jax.named_scope("gather_corner"):
+        corner_row = lax.all_gather(tiles[0, 0], "col", axis=1, tiled=True)
+        corner = lax.all_gather(corner_row, "row", axis=0, tiled=True).astype(jnp.float32)
+
     with jax.named_scope("gather_inputs"):
-        band = lax.all_gather(local[:, : 2 * tile_cols], "col", axis=0)
-        band = band.reshape(col_count, NT * tile_rows, 2, tile_cols)
-        band = band.transpose(1, 2, 0, 3).reshape(NT * tile_rows, 2 * P_SIZE)
-        own_rows = band[tile_rows:].astype(jnp.float32)
-        top = jnp.concatenate([band[: 2 * tile_rows], local[: 2 * tile_rows, 2 * tile_cols :]], axis=1)
-        top = lax.all_gather(top, "row", axis=0)
-        top = top.reshape(row_count, 2, tile_rows, top.shape[-1]).transpose(1, 0, 2, 3)
-        top = top.reshape(2 * P_SIZE, top.shape[-1]).astype(jnp.float32)
-        corners = jnp.stack(
-            [top[:P_SIZE, :P_SIZE], top[P_SIZE:, :P_SIZE], top[P_SIZE : 2 * P_SIZE, P_SIZE : 2 * P_SIZE]]
-        )
-        own_second = lax.dynamic_slice_in_dim(top, P_SIZE + column_index * tile_cols, tile_cols, 1)
-        col_rows = jnp.concatenate([own_second, top[:, 2 * P_SIZE :]], axis=1).T
+        own_rows = lax.all_gather(local[tile_rows:, : 2 * tile_cols], "col", axis=0)
+        own_rows = own_rows.reshape(col_count, (NT - 1) * tile_rows, 2, tile_cols)
+        own_rows = own_rows.transpose(1, 2, 0, 3).reshape((NT - 1) * tile_rows, 2 * P_SIZE)
+        next_band = lax.all_gather(own_rows[:tile_rows], "row", axis=0, tiled=True)
+        own_rows = own_rows.astype(jnp.float32)
+        next_band = next_band.astype(jnp.float32)
+        col_rows = lax.all_gather(local[: 2 * tile_rows, tile_cols:], "row", axis=0)
+        col_rows = col_rows.reshape(row_count, 2, tile_rows, (NT - 1) * tile_cols)
+        col_rows = col_rows.transpose(3, 1, 0, 2).reshape((NT - 1) * tile_cols, 2 * P_SIZE)
+        col_rows = col_rows.astype(jnp.float32)
 
     with jax.named_scope("first_panel"):
-        first_factor, first_inverse = factor_and_inverse(0.5 * (corners[0] + corners[0].T))
+        first_factor, first_inverse = factor_and_inverse(0.5 * (corner + corner.T))
         own_count = (NT - 1) * tile_rows
-        col_total = (NT - 1) * tile_cols
         stacked = jnp.concatenate(
-            [corners[1], own_rows[:, :P_SIZE], col_rows[:, :P_SIZE]], axis=0
+            [next_band[:, :P_SIZE], own_rows[:, :P_SIZE], col_rows[:, :P_SIZE]], axis=0
         )
         solved = exact_dot(stacked, first_inverse)
         next_rows = solved[:P_SIZE].astype(jnp.bfloat16)
@@ -144,7 +144,7 @@
         first_col = solved[P_SIZE + own_count :]
 
     with jax.named_scope("second_panel"):
-        second_corner = corners[2] - bf16_gram(next_rows, next_rows)
+        second_corner = next_band[:, P_SIZE:] - bf16_gram(next_rows, next_rows)
         second_factor, second_inverse = factor_and_inverse(0.5 * (second_corner + second_corner.T))
         own_below = own_rows[tile_rows:, P_SIZE:] - bf16_gram(first_own[tile_rows:], next_rows)
         col_below = col_rows[tile_cols:, P_SIZE:] - bf16_gram(first_col[tile_cols:], next_rows)

time: 330 us -> 346 us (1.048)
  blocking collectives: 35.4 us -> 117 us
  waiting for transfers between devices: 60.9 us -> 0.02 us
  other arithmetic: 11.5 us -> 5.09 us
  matrix products: 14 us -> 19.9 us
  local copies, waits for them, and re-layouts: 35.5 us -> 31.8 us
    all_gather x1 -> x4, blocking collectives: 35.4 us -> 117 us  [the longest x1 40.1 us: per_device(): lax.all_gather(corner_row, 'row', axis=0, tiled=True).astype(jnp.float32)]
    all_gather x1, waiting for transfers between devices: 60.9 us -> 0.01 us  [per_device(): next_band = lax.all_gather(own_rows[:tile_rows], 'row', axis=0, tiled=True)]
    unnamed x17 -> x18, local copies, waits for them, and re-layouts: 10.4 us -> 3.57 us
    dot_general x2, matrix products: 9.99 us -> 16.5 us  [exact_dot(): lax.dot_general(left_side, right_side, (((1,), (1,)), ((), ())), precisio...]
    slice x1 -> x0, other arithmetic: 3.77 us -> none  [per_device(): top[P_SIZE:2 * P_SIZE, P_SIZE:2 * P_SIZE]]
  transfers between devices with their start and end apart: 1 -> 1, of which waited for: 1 -> 0; matrix products, arithmetic and copies ran while one was open for 1% -> 2% of each run, Pallas kernels for 0% -> 23%
where the time goes in v1:
time: 346 us
  Pallas kernels  158 us (46%)
  blocking collectives  117 us (34%)
  local copies, waits for them, and re-layouts  31.8 us (9%)
  matrix products  19.9 us (6%)
  between operations  13.7 us (4%)
  other arithmetic  5.09 us (1%)
    pallas_call x2, Pallas kernels, factor_and_inverse(): pl.pallas_call(factor_kernel, out_shape=(jax.ShapeDtypeStruct((size, size...  158 us
    all_gather x1, blocking collectives, per_device(): lax.all_gather(corner_row, 'row', axis=0, tiled=True).astype(jnp.float32)  40.1 us
    all_gather x1, blocking collectives, per_device(): own_rows = lax.all_gather(local[tile_rows:, :2 * tile_cols], 'col', axis=0)  31.8 us
    all_gather x1, blocking collectives, per_device(): col_rows = lax.all_gather(local[:2 * tile_rows, tile_cols:], 'row', axis=0)  24.3 us
    all_gather x1, blocking collectives, per_device(): corner_row = lax.all_gather(tiles[0, 0], 'col', axis=1, tiled=True)  20.4 us
    dot_general x2, matrix products, exact_dot(): lax.dot_general(left_side, right_side, (((1,), (1,)), ((), ())), precisio...  16.5 us
  transfers between devices with their start and end apart: 1, of which 0 were waited for; matrix products, arithmetic and copies ran while one was open for 2% of the time, Pallas kernels for 23%

profile of v1, /device:TPU:1, one launch (start us, length us, event | category | flops | bytes accessed | tf_op | source)
XLA Modules:
  0.0 345.5 jit_solution(16752330922411829840)
XLA Ops:
  6.5 1.7 reshape.174
  9.7 31.8 %all-gather.4 = bf16[16,240,64]{1,2,0:T(8,128)(2,1)S(1)} all-gather(bf16[1,240,64]{1,2,0:T(8,128)(2,1)S(1)} %copy.48), channel_id=4, replica_groups=mesh['row'=32,'col'=16] {'col'}, dimensions={0}, use_global_device_ids=true | all-gather | bytes 522240 | tf_op jit(solution)/shard_map/gather_inputs/all_gather | solution.py:124
  42.9 20.4 %all-gather = bf16[1,1,16,512]{2,1,0,3:T(2,128)(2,1)S(1)} all-gather(bf16[1,1,16,32]{2,1,0,3:T(2,128)(2,1)S(1)} %copy.43), channel_id=2, replica_groups=mesh['row'=32,'col'=16] {'col'}, dimensions={3}, use_global_device_ids=true | all-gather | bytes 17408 | tf_op jit(solution)/shard_map/gather_corner/all_gather | solution.py:120
  63.4 40.1 %all-gather.1 = bf16[1,1,512,512]{3,2,1,0:T(8,128)(2,1)S(1)} all-gather(bf16[1,1,16,512]{3,2,1,0:T(8,128)(2,1)S(1)} %copy.44), channel_id=3, replica_groups=mesh['row'=32,'col'=16] {'row'}, dimensions={2}, use_global_device_ids=true | all-gather | bytes 540672 | tf_op jit(solution)/shard_map/gather_corner/all_gather | solution.py:121
  103.7 1.1 bitcast_convert_fusion
  104.9 1.6 copy.46
  106.4 1.1 fusion.5.sym_ref
  107.6 79.1 %first_panel.1 = (f32[512,512]{1,0:T(8,128)}, f32[512,512]{1,0:T(8,128)}) custom-call(f32[512,512]{1,0:T(8,128)} %fusion.5.sym_ref), custom_call_target="tpu_custom_call" | custom-call | tf_op jit(solution)/shard_map/first_panel/pallas_call | solution.py:90
  186.7 24.3 %all-gather.3 = bf16[1024,480]{1,0:T(8,128)(2,1)S(1)} all-gather(bf16[32,480]{1,0:T(8,128)(2,1)S(1)} %slice.196), channel_id=5, replica_groups=mesh['row'=32,'col'=16] {'row'}, dimensions={0}, use_global_device_ids=true | all-gather | bytes 1013760 | tf_op jit(solution)/shard_map/gather_inputs/all_gather | solution.py:130
  211.2 1.3 copy-done
  215.3 1.5 copy.50
  216.8 1.1 slice.194
  217.9 1.6 convert_element_type.37
  219.5 2.7 concatenate.16
  222.3 9.8 %fusion.16 = (bf16[1232,512]{1,0:T(8,128)(2,1)S(1)}, f32[1232,512]{1,0:T(8,128)S(1)}) fusion(f32[1232,512]{0,1:T(8,128)S(1)} %concatenate.16, f32[512,512]{1,0:T(8,128)} %get-tuple-element.70), kind=kOutput, calls=%fused_computation.28 | convolution fusion | flops 3876167680 | bytes 7356416 | tf_op jit(solution)/shard_map/first_panel/dot_general | solution.py:26
  233.3 1.1 convolution_subtract_fusion.2
  237.0 1.2 fusion.4.sym_ref
  238.2 79.3 %second_panel.1 = (f32[512,512]{1,0:T(8,128)}, f32[512,512]{1,0:T(8,128)}) custom-call(f32[512,512]{1,0:T(8,128)} %fusion.4.sym_ref), custom_call_target="tpu_custom_call" | custom-call | tf_op jit(solution)/shard_map/second_panel/pallas_call | solution.py:90
  318.3 6.7 %fusion = f32[672,512]{1,0:T(8,128)S(1)} fusion(f32[512,512]{1,0:T(8,128)} %get-tuple-element.72, f32[448,512]{0,1:T(8,128)S(1)} %convolution_subtract_fusion, f32[224,512]{0,1:T(8,128)S(1)} %copy-done.5), kind=kOutput, calls=%fused_computation | convolution fusion | flops 2114273280 | bytes 3801088 | tf_op jit(solution)/shard_map/second_panel/dot_general | solution.py:26
  326.3 1.7 scatter.19
  329.0 2.1 scatter.21
  331.2 1.8 scatter.24
  333.5 2.0 copy.57
  335.5 3.1 reshape.178
  (48 shorter events, 13.4 us)
Async XLA Ops:
  6.5 208.7 %all-gather.7.cloned.1.call-start = ((), (), s32[]{:S(2)}) async-start(), calls=%async_computation | async-start | bytes 1081344 | tf_op jit(solution)/shard_map/gather_inputs/all_gather | solution.py:127
  42.7 143.9 %copy-start.3 = (f32[240,2,16,32]{0,3,2,1:T(8,128)}, f32[240,2,16,32]{0,3,2,1:T(8,128)S(1)}, u32[]{:S(2)}) copy-start(f32[240,2,16,32]{0,3,2,1:T(8,128)S(1)} %copy.51) | copy-start | bytes 2949124
  211.2 1.3 copy-start
  222.2 9.8 %copy-start.1 = (f32[32,2,16,480]{3,2,0,1:T(8,128)S(1)}, f32[32,2,16,480]{3,2,0,1:T(8,128)}, u32[]{:S(2)}) copy-start(f32[32,2,16,480]{3,2,0,1:T(8,128)} %copy-done) | copy-start | bytes 5898244
  232.1 1.2 copy-start.4
  234.4 1.8 copy-start.2
  238.2 80.1 %copy-start.5 = (f32[224,512]{0,1:T(8,128)S(1)}, f32[224,512]{0,1:T(8,128)}, u32[]{:S(2)}) copy-start(f32[224,512]{0,1:T(8,128)} %convolution_subtract_fusion.2) | copy-start | bytes 1376260
  325.0 1.0 copy-start.7
  325.0 1.3 copy-start.6
Sparse Core Ops, SparseCore 0:
  42.7 61.8 all-gather.6

commit v2 on v0

--- a/solution.py
+++ b/solution.py
@@ -1,3 +1,4 @@
+import functools
 import jax
 import jax.numpy as jnp
 from jax import lax
@@ -106,6 +107,51 @@
     )(sym)
 
 
+MESH_IDS = pl.DeviceIdType.MESH
+
+
+def spread_kernel(axis, count, piece_ref, out_ref, send_sem, recv_sem):
+    me = lax.axis_index(axis)
+    barrier = pltpu.get_barrier_semaphore()
+    for offset in range(1, count):
+        peer = lax.rem(me + offset, count)
+        pl.semaphore_signal(barrier, inc=1, device_id={axis: peer}, device_id_type=MESH_IDS)
+    pl.semaphore_wait(barrier, count - 1)
+    sends = []
+    for offset in range(1, count):
+        peer = lax.rem(me + offset, count)
+        copy = pltpu.make_async_remote_copy(
+            src_ref=piece_ref, dst_ref=out_ref.at[me],
+            send_sem=send_sem.at[offset], recv_sem=recv_sem.at[offset],
+            device_id={axis: peer}, device_id_type=MESH_IDS,
+        )
+        copy.start()
+        sends.append(copy)
+    out_ref[me] = piece_ref[...]
+    for copy in sends:
+        copy.wait_send()
+    for offset in range(1, count):
+        source = lax.rem(me + count - offset, count)
+        arrival = pltpu.make_async_remote_copy(
+            src_ref=piece_ref, dst_ref=out_ref.at[source],
+            send_sem=send_sem.at[offset], recv_sem=recv_sem.at[offset],
+            device_id={axis: source}, device_id_type=MESH_IDS,
+        )
+        arrival.wait_recv()
+
+
+def spread(piece, axis, key):
+    count = lax.axis_size(axis)
+    return pl.pallas_call(
+        functools.partial(spread_kernel, axis, count),
+        out_shape=jax.ShapeDtypeStruct((count,) + piece.shape, piece.dtype),
+        in_specs=[pl.BlockSpec(memory_space=pltpu.VMEM)],
+        out_specs=pl.BlockSpec(memory_space=pltpu.VMEM),
+        scratch_shapes=[pltpu.SemaphoreType.DMA((count,)), pltpu.SemaphoreType.DMA((count,))],
+        compiler_params=pltpu.CompilerParams(collective_id=key, has_side_effects=True),
+    )(piece)
+
+
 def per_device(kernel):
     row_count = lax.axis_size("row")
     col_count = lax.axis_size("col")
@@ -117,12 +163,12 @@
     local = tiles.transpose(0, 2, 1, 3).reshape(NT * tile_rows, NT * tile_cols)
 
     with jax.named_scope("gather_inputs"):
-        band = lax.all_gather(local[:, : 2 * tile_cols], "col", axis=0)
+        band = spread(local[:, : 2 * tile_cols], "col", 0)
         band = band.reshape(col_count, NT * tile_rows, 2, tile_cols)
         band = band.transpose(1, 2, 0, 3).reshape(NT * tile_rows, 2 * P_SIZE)
         own_rows = band[tile_rows:].astype(jnp.float32)
         top = jnp.concatenate([band[: 2 * tile_rows], local[: 2 * tile_rows, 2 * tile_cols :]], axis=1)
-        top = lax.all_gather(top, "row", axis=0)
+        top = spread(top, "row", 1)
         top = top.reshape(row_count, 2, tile_rows, top.shape[-1]).transpose(1, 0, 2, 3)
         top = top.reshape(2 * P_SIZE, top.shape[-1]).astype(jnp.float32)
         corners = jnp.stack(

time: 330 us -> 344 us (1.042)
  Pallas kernels: 158 us -> 283 us
  waiting for transfers between devices: 60.9 us -> 0 us
  blocking collectives: 35.4 us -> 0 us
  between operations: 13.7 us -> 0.32 us
  other arithmetic: 11.5 us -> 7.61 us
    pallas_call x0 -> x2, Pallas kernels: none -> 124 us  [spread(): pl.pallas_call(functools.partial(spread_kernel, axis, count), out_shape=j...]
    all_gather x1 -> x0, waiting for transfers between devices: 60.9 us -> none  [per_device(): top = lax.all_gather(top, 'row', axis=0)]
    all_gather x1 -> x0, blocking collectives: 35.4 us -> none  [per_device(): band = lax.all_gather(local[:, :2 * tile_cols], 'col', axis=0)]
    unnamed x17, local copies, waits for them, and re-layouts: 10.4 us -> 6.73 us
  transfers between devices with their start and end apart: 1 -> 0, of which waited for: 1 -> 0; matrix products, arithmetic and copies ran while one was open for 1% -> 0% of each run, Pallas kernels for 0% -> 0%
where the time goes in v2:
time: 344 us; the launch traced here: 343 us
  Pallas kernels  283 us (82%)
  local copies, waits for them, and re-layouts  35.3 us (10%)
  matrix products  17.1 us (5%)
  other arithmetic  7.61 us (2%)
    pallas_call x2, Pallas kernels, factor_and_inverse(): pl.pallas_call(factor_kernel, out_shape=(jax.ShapeDtypeStruct((size, size...  159 us
    pallas_call x2, Pallas kernels, spread(): pl.pallas_call(functools.partial(spread_kernel, axis, count), out_shape=j...  124 us
    dot_general x2, matrix products, exact_dot(): lax.dot_general(left_side, right_side, (((1,), (1,)), ((), ())), precisio...  13.1 us

profile of v2, /device:TPU:1, one launch (start us, length us, event | category | flops | bytes accessed | tf_op | source)
XLA Modules:
  0.0 343.0 jit_solution(7902029384899658194)
XLA Ops:
  0.0 1.7 reshape.175
  3.7 63.7 %gather_inputs.2 = bf16[16,256,64]{2,1,0:T(8,128)(2,1)} custom-call(bf16[256,64]{1,0:T(8,128)(2,1)} %slice.200.piece_ref), custom_call_target="tpu_custom_call" | custom-call | tf_op jit(solution)/shard_map/gather_inputs/pallas_call | solution.py:145
  67.4 1.5 copy.13
  70.5 60.3 %gather_inputs.3 = bf16[32,32,1472]{2,1,0:T(8,128)(2,1)} custom-call(bf16[32,1472]{1,0:T(8,128)(2,1)} %pad_maximum_fusion.piece_ref), custom_call_target="tpu_custom_call" | custom-call | tf_op jit(solution)/shard_map/gather_inputs/pallas_call | solution.py:145
  130.9 2.8 copy.15
  134.7 1.7 copy-done
  136.4 1.3 copy.20
  137.7 2.3 slice.203
  140.0 1.6 copy.26
  141.5 3.8 %fusion.23 = (f32[512,512]{1,0:T(8,128)}, f32[512,512]{1,0:T(8,128)}, f32[512,512]{1,0:T(8,128)}) fusion(f32[1024,1472]{1,0:T(8,128)} %bitcast.38, f32[512,512]{0,1:T(8,128)S(1)} %copy.26), kind=kLoop, calls=%fused_computation.38 | loop fusion | flops 524288 | bytes 7340032 | tf_op jit(solution)/shard_map/gather_inputs/slice | solution.py:175
  145.3 79.3 %first_panel.1 = (f32[512,512]{1,0:T(8,128)}, f32[512,512]{1,0:T(8,128)}) custom-call(f32[512,512]{1,0:T(8,128)} %get-tuple-element.74.sym_ref), custom_call_target="tpu_custom_call" | custom-call | tf_op jit(solution)/shard_map/first_panel/pallas_call | solution.py:91
  224.6 1.3 slice_convert_fusion.1
  227.9 7.6 %fusion.24 = (bf16[1232,512]{1,0:T(8,128)(2,1)S(1)}, f32[1232,512]{1,0:T(8,128)}) fusion(f32[512,512]{1,0:T(8,128)} %get-tuple-element.70, f32[480,512]{1,0:T(8,128)} %copy.20, f32[240,512]{1,0:T(8,128)} %copy.27, f32[512,512]{1,0:T(8,128)} %get-tuple-element.75), kind=kOutput, calls=%fused_computation.39 | convolution fusion | flops 3877429248 | bytes 7356416 | tf_op jit(solution)/shard_map/first_panel/dot_general | solution.py:27
  235.6 1.5 convolution_subtract_fusion
  237.1 1.6 copy.28
  239.4 1.3 fusion.10.sym_ref
  240.7 79.3 %second_panel.1 = (f32[512,512]{1,0:T(8,128)}, f32[512,512]{1,0:T(8,128)}) custom-call(f32[512,512]{1,0:T(8,128)} %fusion.10.sym_ref), custom_call_target="tpu_custom_call" | custom-call | tf_op jit(solution)/shard_map/second_panel/pallas_call | solution.py:91
  320.1 1.5 convolution_subtract_fusion.2
  321.6 5.5 %fusion.6 = f32[672,512]{1,0:T(8,128)S(1)} fusion(f32[512,512]{1,0:T(8,128)S(1)} %copy-done.6, f32[448,512]{0,1:T(8,128)S(1)} %copy-done.2, f32[224,512]{0,1:T(8,128)S(1)} %convolution_subtract_fusion.2), kind=kOutput, calls=%fused_computation.7 | convolution fusion | flops 2114273280 | bytes 3801088 | tf_op jit(solution)/shard_map/second_panel/dot_general | solution.py:27
  330.7 1.7 scatter.19
  333.4 2.1 scatter.21
  335.5 1.8 scatter.24
  337.9 2.0 copy.24
  339.9 3.1 reshape.179
  (41 shorter events, 12.5 us)
Async XLA Ops:
  3.0 66.8 %copy-start.4 = (bf16[256,512]{1,0:T(8,128)(2,1)}, bf16[256,512]{1,0:T(8,128)(2,1)S(1)}, u32[]{:S(2)}) copy-start(bf16[256,512]{1,0:T(8,128)(2,1)S(1)} %reshape.176) | copy-start | bytes 786436
  69.0 61.9 %copy-start.3 = (bf16[16,256,64]{1,2,0:T(8,128)(2,1)}, bf16[16,256,64]{1,2,0:T(8,128)(2,1)S(1)}, u32[]{:S(2)}) copy-start(bf16[16,256,64]{1,2,0:T(8,128)(2,1)S(1)} %copy.13) | copy-start | bytes 1572868
  133.6 2.7 copy-start
  225.9 1.0 copy-start.1
  240.7 80.8 %copy-start.2 = (f32[448,512]{0,1:T(8,128)S(1)}, f32[448,512]{0,1:T(8,128)}, u32[]{:S(2)}) copy-start(f32[448,512]{0,1:T(8,128)} %convolution_subtract_fusion) | copy-start | bytes 2752516
  320.1 1.5 copy-start.6
  321.6 5.5 %copy-start.5 = (bf16[256,512]{1,0:T(8,128)(2,1)S(1)}, bf16[256,512]{1,0:T(8,128)(2,1)}, u32[]{:S(2)}) copy-start(bf16[256,512]{1,0:T(8,128)(2,1)} %copy-done.4) | copy-start | bytes 786436

commit v3 on v0

--- a/solution.py
+++ b/solution.py
@@ -45,22 +45,46 @@
         diag_ref[...] = jnp.zeros((BLOCK, BLOCK), jnp.float32)
         dinv_ref[...] = eye
 
-        def step(j, block):
-            col = jnp.sum(jnp.where(lanes == j, block, 0.0), axis=1, keepdims=True)
-            row = jnp.sum(jnp.where(rows == j, block, 0.0), axis=0, keepdims=True)
-            pivot = jnp.sum(jnp.where(col_ids == j, col, 0.0), axis=0, keepdims=True)
-            root = jnp.sqrt(pivot)
-            scale = 1.0 / root
-            c_col = jnp.where(col_ids > j, col * scale, jnp.where(col_ids == j, root, 0.0))
-            c_row = jnp.where(row_ids > j, row * scale, jnp.where(row_ids == j, root, 0.0))
-            diag_ref[...] = jnp.where(lanes == j, c_col, diag_ref[...])
+        def pick_col(block, at):
+            return jnp.sum(jnp.where(lanes == at, block, 0.0), axis=1, keepdims=True)
+
+        def pick_row(block, at):
+            return jnp.sum(jnp.where(rows == at, block, 0.0), axis=0, keepdims=True)
+
+        def entry(vector, at):
+            return jnp.sum(jnp.where(col_ids == at, vector, 0.0), axis=0, keepdims=True)
+
+        def step(half, block):
+            j = 2 * half
+            k = j + 1
+            col_j = pick_col(block, j)
+            col_k = pick_col(block, k)
+            row_j = pick_row(block, j)
+            row_k = pick_row(block, k)
+            root_j = jnp.sqrt(entry(col_j, j))
+            scale_j = 1.0 / root_j
+            cross = entry(col_j, k) * scale_j
+            root_k = jnp.sqrt(entry(col_k, k) - cross * cross)
+            scale_k = 1.0 / root_k
+            c_col_j = jnp.where(col_ids > j, col_j * scale_j, jnp.where(col_ids == j, root_j, 0.0))
+            c_row_j = jnp.where(row_ids > j, row_j * scale_j, jnp.where(row_ids == j, root_j, 0.0))
+            c_col_k = jnp.where(
+                col_ids > k, (col_k - c_col_j * cross) * scale_k, jnp.where(col_ids == k, root_k, 0.0)
+            )
+            c_row_k = jnp.where(
+                row_ids > k, (row_k - c_row_j * cross) * scale_k, jnp.where(row_ids == k, root_k, 0.0)
+            )
+            diag_ref[...] = jnp.where(
+                lanes == j, c_col_j, jnp.where(lanes == k, c_col_k, diag_ref[...])
+            )
             inverse = dinv_ref[...]
-            inv_row = jnp.sum(jnp.where(rows == j, inverse, 0.0), axis=0, keepdims=True)
-            shift = jnp.where(col_ids == j, (root - 1.0) * scale, c_col * scale)
-            dinv_ref[...] = inverse - shift * inv_row
-            return block - c_col * c_row
-
-        lax.fori_loop(0, BLOCK, step, work_ref[here, here])
+            shift_j = c_col_j * scale_j - jnp.where(col_ids == j, scale_j, 0.0)
+            inverse = inverse - shift_j * pick_row(inverse, j)
+            shift_k = c_col_k * scale_k - jnp.where(col_ids == k, scale_k, 0.0)
+            dinv_ref[...] = inverse - shift_k * pick_row(inverse, k)
+            return block - c_col_j * c_row_j - c_col_k * c_row_k
+
+        lax.fori_loop(0, BLOCK // 2, step, work_ref[here, here], unroll=2)
         low_ref[here, here] = diag_ref[...]
         inv_ref[here, here] = dinv_ref[...]
         if k + 1 < blocks:

time: 330 us -> 286 us (0.87)
  Pallas kernels: 158 us -> 115 us
    pallas_call x2, Pallas kernels: 158 us -> 115 us  [factor_and_inverse(): pl.pallas_call(factor_kernel, out_shape=(jax.ShapeDtypeStruct((size, size...]
where the time goes in v3:
time: 286 us
  Pallas kernels  115 us (40%)
  waiting for transfers between devices  60.9 us (21%)
  local copies, waits for them, and re-layouts  35.5 us (12%)
  blocking collectives  35.4 us (12%)
  matrix products  14 us (5%)
  between operations  13.7 us (5%)
  other arithmetic  11.5 us (4%)
    pallas_call x2, Pallas kernels, factor_and_inverse(): pl.pallas_call(factor_kernel, out_shape=(jax.ShapeDtypeStruct((size, size...  115 us
    all_gather x1, waiting for transfers between devices, per_device(): top = lax.all_gather(top, 'row', axis=0)  60.9 us
    all_gather x1, blocking collectives, per_device(): band = lax.all_gather(local[:, :2 * tile_cols], 'col', axis=0)  35.4 us
    unnamed x17, local copies, waits for them, and re-layouts  10.4 us
    dot_general x2, matrix products, exact_dot(): lax.dot_general(left_side, right_side, (((1,), (1,)), ((), ())), precisio...  9.99 us
  transfers between devices with their start and end apart: 1, of which 1 were waited for; matrix products, arithmetic and copies ran while one was open for 1% of the time, Pallas kernels for 0%

profile of v3, /device:TPU:1, one launch (start us, length us, event | category | flops | bytes accessed | tf_op | source)
XLA Modules:
  0.0 285.6 jit_solution(8357310048246526055)
XLA Ops:
  6.5 1.7 reshape.175
  9.6 35.4 %all-gather = bf16[4096,64]{1,0:T(8,128)(2,1)S(1)} all-gather(bf16[256,64]{1,0:T(8,128)(2,1)S(1)} %slice.200), channel_id=2, replica_groups=mesh['row'=32,'col'=16] {'col'}, dimensions={0}, use_global_device_ids=true | all-gather | bytes 557056 | tf_op jit(solution)/shard_map/gather_inputs/all_gather | solution.py:144
  50.1 60.9 %all-gather.4.cloned.1.call-done = bf16[1024,1472]{1,0:T(8,128)(2,1)} async-done(((bf16[32,1472]{1,0:T(8,128)(2,1)}), bf16[1024,1472]{1,0:T(8,128)(2,1)}) %all-gather.4.cloned.1.call-update) | async-done | bytes 3014672 | tf_op jit(solution)/shard_map/gather_inputs/all_gather | solution.py:149
  111.0 2.8 convert_bitcast_fusion
  114.8 1.3 slice.203
  116.1 1.6 copy-done
  118.0 2.0 copy.42
  120.0 1.6 maximum_bitcast_fusion
  122.6 1.6 copy.39
  124.2 3.8 %fusion.23 = (f32[512,512]{1,0:T(8,128)}, f32[512,512]{1,0:T(8,128)}, f32[512,512]{1,0:T(8,128)}) fusion(f32[1024,1472]{1,0:T(8,128)} %bitcast.42, f32[512,512]{0,1:T(8,128)S(1)} %copy.39), kind=kLoop, calls=%fused_computation.39 | loop fusion | flops 524288 | bytes 7340032 | tf_op jit(solution)/shard_map/gather_inputs/slice | solution.py:153
  128.0 57.1 %first_panel.1 = (f32[512,512]{1,0:T(8,128)}, f32[512,512]{1,0:T(8,128)}) custom-call(f32[512,512]{1,0:T(8,128)} %get-tuple-element.74.sym_ref), custom_call_target="tpu_custom_call" | custom-call | tf_op jit(solution)/shard_map/first_panel/pallas_call | solution.py:114
  185.1 7.6 %fusion.24 = (bf16[1232,512]{1,0:T(8,128)(2,1)S(1)}, f32[1232,512]{1,0:T(8,128)}) fusion(f32[512,512]{1,0:T(8,128)} %get-tuple-element.70, f32[480,512]{1,0:T(8,128)} %slice.208, f32[240,512]{1,0:T(8,128)} %copy.40, f32[512,512]{1,0:T(8,128)} %get-tuple-element.75), kind=kOutput, calls=%fused_computation.40 | convolution fusion | flops 3877429248 | bytes 7356416 | tf_op jit(solution)/shard_map/first_panel/dot_general | solution.py:26
  192.7 1.4 convolution_subtract_fusion.1
  195.3 1.3 copy.43
  196.6 1.7 convolution_subtract_fusion
  198.3 1.3 copy.35
  199.7 2.5 fusion.10.sym_ref
  202.2 57.4 %second_panel.1 = (f32[512,512]{1,0:T(8,128)}, f32[512,512]{1,0:T(8,128)}) custom-call(f32[512,512]{1,0:T(8,128)} %fusion.10.sym_ref), custom_call_target="tpu_custom_call" | custom-call | tf_op jit(solution)/shard_map/second_panel/pallas_call | solution.py:114
  260.8 2.4 fusion.6
  266.5 1.7 scatter.19
  269.2 2.1 scatter.21
  271.3 1.8 scatter.24
  273.7 2.0 copy.37
  275.7 3.1 %reshape.179 = f32[16,1,16,1,512]{4,3,2,1,0:T(1,128)} reshape(f32[16,16,16,32]{3,2,1,0:T(8,128)} %copy.37) | data formatting | bytes 1048576 | tf_op jit(solution)/shard_map/reshape | solution.py:200
  (44 shorter events, 15.8 us)
Async XLA Ops:
  6.5 104.4 %all-gather.4.cloned.1.call-start = ((), (), s32[]{:S(2)}) async-start(), calls=%async_computation | async-start | bytes 3244032 | tf_op jit(solution)/shard_map/gather_inputs/all_gather | solution.py:149
  114.6 3.1 %copy-start = (f32[2,32,16,1472]{3,2,1,0:T(8,128)}, f32[2,32,16,1472]{3,2,1,0:T(8,128)S(1)}, u32[]{:S(2)}) copy-start(f32[2,32,16,1472]{3,2,1,0:T(8,128)S(1)} %copy.26) | copy-start | bytes 18087940
  194.1 1.2 copy-start.1
  199.7 59.9 %copy-start.3 = (f32[224,512]{1,0:T(8,128)S(1)}, f32[224,512]{1,0:T(8,128)}, u32[]{:S(2)}) copy-start(f32[224,512]{1,0:T(8,128)} %copy.44) | copy-start | bytes 1376260
  202.2 57.7 %copy-start.2 = (f32[448,512]{1,0:T(8,128)S(1)}, f32[448,512]{1,0:T(8,128)}, u32[]{:S(2)}) copy-start(f32[448,512]{1,0:T(8,128)} %convolution_subtract_fusion.1) | copy-start | bytes 2752516
  259.6 1.2 copy-start.4
Sparse Core Ops, SparseCore 0:
  47.1 63.7 all-gather.3

commit v4 on v3

--- a/solution.py
+++ b/solution.py
@@ -145,22 +145,22 @@
         band = band.reshape(col_count, NT * tile_rows, 2, tile_cols)
         band = band.transpose(1, 2, 0, 3).reshape(NT * tile_rows, 2 * P_SIZE)
         own_rows = band[tile_rows:].astype(jnp.float32)
+        corner = lax.all_gather(band[:tile_rows, :P_SIZE], "row", axis=0, tiled=True)
+        corner = corner.astype(jnp.float32)
         top = jnp.concatenate([band[: 2 * tile_rows], local[: 2 * tile_rows, 2 * tile_cols :]], axis=1)
         top = lax.all_gather(top, "row", axis=0)
         top = top.reshape(row_count, 2, tile_rows, top.shape[-1]).transpose(1, 0, 2, 3)
         top = top.reshape(2 * P_SIZE, top.shape[-1]).astype(jnp.float32)
-        corners = jnp.stack(
-            [top[:P_SIZE, :P_SIZE], top[P_SIZE:, :P_SIZE], top[P_SIZE : 2 * P_SIZE, P_SIZE : 2 * P_SIZE]]
-        )
+        corners = jnp.stack([top[P_SIZE:, :P_SIZE], top[P_SIZE : 2 * P_SIZE, P_SIZE : 2 * P_SIZE]])
         own_second = lax.dynamic_slice_in_dim(top, P_SIZE + column_index * tile_cols, tile_cols, 1)
         col_rows = jnp.concatenate([own_second, top[:, 2 * P_SIZE :]], axis=1).T
 
     with jax.named_scope("first_panel"):
-        first_factor, first_inverse = factor_and_inverse(0.5 * (corners[0] + corners[0].T))
+        first_factor, first_inverse = factor_and_inverse(0.5 * (corner + corner.T))
         own_count = (NT - 1) * tile_rows
         col_total = (NT - 1) * tile_cols
         stacked = jnp.concatenate(
-            [corners[1], own_rows[:, :P_SIZE], col_rows[:, :P_SIZE]], axis=0
+            [corners[0], own_rows[:, :P_SIZE], col_rows[:, :P_SIZE]], axis=0
         )
         solved = exact_dot(stacked, first_inverse)
         next_rows = solved[:P_SIZE].astype(jnp.bfloat16)
@@ -168,7 +168,7 @@
         first_col = solved[P_SIZE + own_count :]
 
     with jax.named_scope("second_panel"):
-        second_corner = corners[2] - bf16_gram(next_rows, next_rows)
+        second_corner = corners[1] - bf16_gram(next_rows, next_rows)
         second_factor, second_inverse = factor_and_inverse(0.5 * (second_corner + second_corner.T))
         own_below = own_rows[tile_rows:, P_SIZE:] - bf16_gram(first_own[tile_rows:], next_rows)
         col_below = col_rows[tile_cols:, P_SIZE:] - bf16_gram(first_col[tile_cols:], next_rows)

time: 286 us -> 249 us (0.87)
  waiting for transfers between devices: 60.9 us -> 0.02 us
  blocking collectives: 35.4 us -> 68.2 us
  other arithmetic: 11.5 us -> 7.66 us
  local copies, waits for them, and re-layouts: 35.5 us -> 32 us
    all_gather x1, waiting for transfers between devices: 60.9 us -> 0.01 us  [per_device(): top = lax.all_gather(top, 'row', axis=0)]
    all_gather x0 -> x1, blocking collectives: none -> 32.7 us  [per_device(): lax.all_gather(band[:tile_rows, :P_SIZE], 'row', axis=0, tiled=True)]
    slice x1 -> x0, other arithmetic: 3.77 us -> none  [per_device(): top[P_SIZE:2 * P_SIZE, P_SIZE:2 * P_SIZE]]
    unnamed x17 -> x20, local copies, waits for them, and re-layouts: 10.4 us -> 6.71 us
  transfers between devices with their start and end apart: 1 -> 1, of which waited for: 1 -> 0; matrix products, arithmetic and copies ran while one was open for 1% -> 3% of each run, Pallas kernels for 0% -> 23%
where the time goes in v4:
time: 249 us
  Pallas kernels  115 us (46%)
  blocking collectives  68.2 us (27%)
  local copies, waits for them, and re-layouts  32 us (13%)
  between operations  13.7 us (6%)
  matrix products  12.7 us (5%)
  other arithmetic  7.66 us (3%)
    pallas_call x2, Pallas kernels, factor_and_inverse(): pl.pallas_call(factor_kernel, out_shape=(jax.ShapeDtypeStruct((size, size...  115 us
    all_gather x1, blocking collectives, per_device(): band = lax.all_gather(local[:, :2 * tile_cols], 'col', axis=0)  35.4 us
    all_gather x1, blocking collectives, per_device(): lax.all_gather(band[:tile_rows, :P_SIZE], 'row', axis=0, tiled=True)  32.7 us
    dot_general x2, matrix products, exact_dot(): lax.dot_general(left_side, right_side, (((1,), (1,)), ((), ())), precisio...  8.02 us
    unnamed x20, local copies, waits for them, and re-layouts  6.71 us
  transfers between devices with their start and end apart: 1, of which 0 were waited for; matrix products, arithmetic and copies ran while one was open for 3% of the time, Pallas kernels for 23%

profile of v4, /device:TPU:1, one launch (start us, length us, event | category | flops | bytes accessed | tf_op | source)
XLA Modules:
  0.0 248.8 jit_solution(9223796506872180559)
XLA Ops:
  6.5 1.7 reshape.177
  9.6 35.4 %all-gather = bf16[4096,64]{1,0:T(8,128)(2,1)S(1)} all-gather(bf16[256,64]{1,0:T(8,128)(2,1)S(1)} %slice.200), channel_id=2, replica_groups=mesh['row'=32,'col'=16] {'col'}, dimensions={0}, use_global_device_ids=true | all-gather | bytes 557056 | tf_op jit(solution)/shard_map/gather_inputs/all_gather | solution.py:144
  48.4 32.7 %all_gather.17 = bf16[512,512]{1,0:T(8,128)(2,1)S(1)} all-gather(bf16[16,512]{1,0:T(8,128)(2,1)S(1)} %copy.57), channel_id=1, replica_groups=mesh['row'=32,'col'=16] {'row'}, dimensions={0}, use_global_device_ids=true | all-gather | bytes 540672 | tf_op jit(solution)/shard_map/gather_inputs/all_gather | solution.py:148
  81.5 1.2 fusion.11.sym_ref
  82.7 57.1 %first_panel.1 = (f32[512,512]{1,0:T(8,128)}, f32[512,512]{1,0:T(8,128)}) custom-call(f32[512,512]{1,0:T(8,128)} %fusion.11.sym_ref), custom_call_target="tpu_custom_call" | custom-call | tf_op jit(solution)/shard_map/first_panel/pallas_call | solution.py:114
  139.8 1.0 copy.72
  143.5 2.8 %convert_bitcast_fusion = f32[2,32,16,1472]{3,2,0,1:T(8,128)S(1)} fusion(bf16[32,2,16,1472]{3,2,1,0:T(8,128)(2,1)} %bitcast.50), kind=kLoop, calls=%fused_computation | loop fusion | flops 1507328 | bytes 9043968 | tf_op jit(solution)/shard_map/gather_inputs/convert_element_type | solution.py:153
  147.2 1.1 fusion.23
  149.4 1.2 copy.73
  150.6 1.8 copy.74
  152.4 1.6 maximum_bitcast_fusion
  155.4 5.7 %fusion.24 = (bf16[1232,512]{1,0:T(8,128)(2,1)S(1)}, f32[1232,512]{1,0:T(8,128)}) fusion(f32[512,512]{1,0:T(8,128)S(1)} %copy-done.5, f32[480,512]{1,0:T(8,128)S(1)} %slice.208, f32[240,512]{1,0:T(8,128)S(1)} %copy-done.3, f32[512,512]{1,0:T(8,128)S(1)} %get-tuple-element.74), kind=kOutput, calls=%fused_computation.40 | convolution fusion | flops 3877429248 | bytes 7356416 | tf_op jit(solution)/shard_map/first_panel/dot_general | solution.py:26
  161.0 1.4 convolution_subtract_fusion.1
  162.4 1.1 convolution_subtract_fusion.3
  164.7 1.2 fusion.10.sym_ref
  165.9 57.4 %second_panel.1 = (f32[512,512]{1,0:T(8,128)}, f32[512,512]{1,0:T(8,128)}) custom-call(f32[512,512]{1,0:T(8,128)} %fusion.10.sym_ref), custom_call_target="tpu_custom_call" | custom-call | tf_op jit(solution)/shard_map/second_panel/pallas_call | solution.py:114
  223.3 1.4 convolution_subtract_fusion.4
  224.8 2.4 fusion.6
  228.5 1.1 slice.209
  229.6 1.7 scatter.19
  232.4 2.1 scatter.21
  234.5 1.8 scatter.24
  236.8 2.0 copy.70
  238.8 3.1 %reshape.182 = f32[16,1,16,1,512]{4,3,2,1,0:T(1,128)} reshape(f32[16,16,16,32]{3,2,1,0:T(8,128)} %copy.70) | data formatting | bytes 1048576 | tf_op jit(solution)/shard_map/reshape | solution.py:200
  (53 shorter events, 14.9 us)
Async XLA Ops:
  6.5 136.9 %all-gather.4.cloned.1.call-start = ((), (), s32[]{:S(2)}) async-start(), calls=%async_computation | async-start | bytes 3244032 | tf_op jit(solution)/shard_map/gather_inputs/all_gather | solution.py:151
  154.0 1.0 copy-start.3
  154.0 1.4 copy-start.5
  161.0 2.5 %copy-start = (f32[512,512]{1,0:T(8,128)S(1)}, f32[512,512]{1,0:T(8,128)}, u32[]{:S(2)}) copy-start(f32[512,512]{1,0:T(8,128)} %get-tuple-element.73) | copy-start | bytes 3145732
  165.9 58.9 %copy-start.1 = (f32[448,512]{1,0:T(8,128)S(1)}, f32[448,512]{1,0:T(8,128)}, u32[]{:S(2)}) copy-start(f32[448,512]{1,0:T(8,128)} %convolution_subtract_fusion.1) | copy-start | bytes 2752516
  223.3 1.5 copy-start.6
  224.8 2.4 copy-start.4
  227.2 2.4 copy-start.2
Sparse Core Ops, SparseCore 0:
  47.1 63.6 all-gather.3

commit v5 on v4

--- a/solution.py
+++ b/solution.py
@@ -19,6 +19,7 @@
 
 
 BLOCK = 128
+GROUP = 4
 EXACT = lax.Precision.HIGHEST
 
 
@@ -54,37 +55,41 @@
         def entry(vector, at):
             return jnp.sum(jnp.where(col_ids == at, vector, 0.0), axis=0, keepdims=True)
 
-        def step(half, block):
-            j = 2 * half
-            k = j + 1
-            col_j = pick_col(block, j)
-            col_k = pick_col(block, k)
-            row_j = pick_row(block, j)
-            row_k = pick_row(block, k)
-            root_j = jnp.sqrt(entry(col_j, j))
-            scale_j = 1.0 / root_j
-            cross = entry(col_j, k) * scale_j
-            root_k = jnp.sqrt(entry(col_k, k) - cross * cross)
-            scale_k = 1.0 / root_k
-            c_col_j = jnp.where(col_ids > j, col_j * scale_j, jnp.where(col_ids == j, root_j, 0.0))
-            c_row_j = jnp.where(row_ids > j, row_j * scale_j, jnp.where(row_ids == j, root_j, 0.0))
-            c_col_k = jnp.where(
-                col_ids > k, (col_k - c_col_j * cross) * scale_k, jnp.where(col_ids == k, root_k, 0.0)
-            )
-            c_row_k = jnp.where(
-                row_ids > k, (row_k - c_row_j * cross) * scale_k, jnp.where(row_ids == k, root_k, 0.0)
-            )
-            diag_ref[...] = jnp.where(
-                lanes == j, c_col_j, jnp.where(lanes == k, c_col_k, diag_ref[...])
-            )
+        group = GROUP
+
+        def step(part, block):
+            base = group * part
+            c_cols = []
+            c_rows = []
+            scales = []
+            raw_cols = []
+            for g in range(group):
+                at = base + g
+                v_col = pick_col(block, at)
+                v_row = pick_row(block, at)
+                for i in range(g):
+                    weight = entry(raw_cols[i], at) * scales[i]
+                    v_col = v_col - c_cols[i] * weight
+                    v_row = v_row - c_rows[i] * weight
+                root = jnp.sqrt(entry(v_col, at))
+                scale = 1.0 / root
+                c_cols.append(jnp.where(col_ids > at, v_col * scale, jnp.where(col_ids == at, root, 0.0)))
+                c_rows.append(jnp.where(row_ids > at, v_row * scale, jnp.where(row_ids == at, root, 0.0)))
+                scales.append(scale)
+                raw_cols.append(v_col)
+            low = diag_ref[...]
             inverse = dinv_ref[...]
-            shift_j = c_col_j * scale_j - jnp.where(col_ids == j, scale_j, 0.0)
-            inverse = inverse - shift_j * pick_row(inverse, j)
-            shift_k = c_col_k * scale_k - jnp.where(col_ids == k, scale_k, 0.0)
-            dinv_ref[...] = inverse - shift_k * pick_row(inverse, k)
-            return block - c_col_j * c_row_j - c_col_k * c_row_k
-
-        lax.fori_loop(0, BLOCK // 2, step, work_ref[here, here], unroll=2)
+            for g in range(group):
+                at = base + g
+                low = jnp.where(lanes == at, c_cols[g], low)
+                shift = c_cols[g] * scales[g] - jnp.where(col_ids == at, scales[g], 0.0)
+                inverse = inverse - shift * pick_row(inverse, at)
+                block = block - c_cols[g] * c_rows[g]
+            diag_ref[...] = low
+            dinv_ref[...] = inverse
+            return block
+
+        lax.fori_loop(0, BLOCK // group, step, work_ref[here, here], unroll=1)
         low_ref[here, here] = diag_ref[...]
         inv_ref[here, here] = dinv_ref[...]
         if k + 1 < blocks:

time: 249 us -> 242 us (0.972)
  Pallas kernels: 115 us -> 108 us
    pallas_call x2, Pallas kernels: 115 us -> 108 us  [factor_and_inverse(): pl.pallas_call(factor_kernel, out_shape=(jax.ShapeDtypeStruct((size, size...]
  transfers between devices with their start and end apart: 1 -> 1, of which waited for: 0 -> 0; matrix products, arithmetic and copies ran while one was open for 3% -> 3% of each run, Pallas kernels for 23% -> 22%
where the time goes in v5:
time: 242 us
  Pallas kernels  108 us (45%)
  blocking collectives  68.2 us (28%)
  local copies, waits for them, and re-layouts  32 us (13%)
  between operations  13.7 us (6%)
  matrix products  12.7 us (5%)
  other arithmetic  7.66 us (3%)
    pallas_call x2, Pallas kernels, factor_and_inverse(): pl.pallas_call(factor_kernel, out_shape=(jax.ShapeDtypeStruct((size, size...  108 us
    all_gather x1, blocking collectives, per_device(): band = lax.all_gather(local[:, :2 * tile_cols], 'col', axis=0)  35.4 us
    all_gather x1, blocking collectives, per_device(): lax.all_gather(band[:tile_rows, :P_SIZE], 'row', axis=0, tiled=True)  32.7 us
    dot_general x2, matrix products, exact_dot(): lax.dot_general(left_side, right_side, (((1,), (1,)), ((), ())), precisio...  8.02 us
    unnamed x20, local copies, waits for them, and re-layouts  6.71 us
  transfers between devices with their start and end apart: 1, of which 0 were waited for; matrix products, arithmetic and copies ran while one was open for 3% of the time, Pallas kernels for 22%

profile of v5, /device:TPU:1, one launch (start us, length us, event | category | flops | bytes accessed | tf_op | source)
XLA Modules:
  0.0 242.0 jit_solution(12222699264131792519)
XLA Ops:
  6.5 1.7 reshape.177
  9.6 35.4 %all-gather = bf16[4096,64]{1,0:T(8,128)(2,1)S(1)} all-gather(bf16[256,64]{1,0:T(8,128)(2,1)S(1)} %slice.200), channel_id=2, replica_groups=mesh['row'=32,'col'=16] {'col'}, dimensions={0}, use_global_device_ids=true | all-gather | bytes 557056 | tf_op jit(solution)/shard_map/gather_inputs/all_gather | solution.py:149
  48.4 32.7 %all_gather.17 = bf16[512,512]{1,0:T(8,128)(2,1)S(1)} all-gather(bf16[16,512]{1,0:T(8,128)(2,1)S(1)} %copy.57), channel_id=1, replica_groups=mesh['row'=32,'col'=16] {'row'}, dimensions={0}, use_global_device_ids=true | all-gather | bytes 540672 | tf_op jit(solution)/shard_map/gather_inputs/all_gather | solution.py:153
  81.5 1.2 fusion.11.sym_ref
  82.7 53.7 %first_panel.1 = (f32[512,512]{1,0:T(8,128)}, f32[512,512]{1,0:T(8,128)}) custom-call(f32[512,512]{1,0:T(8,128)} %fusion.11.sym_ref), custom_call_target="tpu_custom_call" | custom-call | tf_op jit(solution)/shard_map/first_panel/pallas_call | solution.py:119
  136.4 1.0 copy.72
  140.0 2.8 %convert_bitcast_fusion = f32[2,32,16,1472]{3,2,0,1:T(8,128)S(1)} fusion(bf16[32,2,16,1472]{3,2,1,0:T(8,128)(2,1)} %bitcast.50), kind=kLoop, calls=%fused_computation | loop fusion | flops 1507328 | bytes 9043968 | tf_op jit(solution)/shard_map/gather_inputs/convert_element_type | solution.py:158
  143.8 1.1 fusion.23
  146.0 1.2 copy.73
  147.2 1.8 copy.74
  148.9 1.6 maximum_bitcast_fusion
  151.9 5.7 %fusion.24 = (bf16[1232,512]{1,0:T(8,128)(2,1)S(1)}, f32[1232,512]{1,0:T(8,128)}) fusion(f32[512,512]{1,0:T(8,128)S(1)} %copy-done.5, f32[480,512]{1,0:T(8,128)S(1)} %slice.208, f32[240,512]{1,0:T(8,128)S(1)} %copy-done.3, f32[512,512]{1,0:T(8,128)S(1)} %get-tuple-element.74), kind=kOutput, calls=%fused_computation.40 | convolution fusion | flops 3877429248 | bytes 7356416 | tf_op jit(solution)/shard_map/first_panel/dot_general | solution.py:27
  157.6 1.4 convolution_subtract_fusion.1
  159.0 1.1 convolution_subtract_fusion.3
  161.2 1.2 fusion.10.sym_ref
  162.5 54.0 %second_panel.1 = (f32[512,512]{1,0:T(8,128)}, f32[512,512]{1,0:T(8,128)}) custom-call(f32[512,512]{1,0:T(8,128)} %fusion.10.sym_ref), custom_call_target="tpu_custom_call" | custom-call | tf_op jit(solution)/shard_map/second_panel/pallas_call | solution.py:119
  216.5 1.4 convolution_subtract_fusion.4
  218.0 2.4 fusion.6
  221.6 1.1 slice.209
  222.8 1.7 scatter.19
  225.5 2.1 scatter.21
  227.7 1.8 scatter.24
  230.0 2.0 copy.70
  232.0 3.1 %reshape.182 = f32[16,1,16,1,512]{4,3,2,1,0:T(1,128)} reshape(f32[16,16,16,32]{3,2,1,0:T(8,128)} %copy.70) | data formatting | bytes 1048576 | tf_op jit(solution)/shard_map/reshape | solution.py:205
  (53 shorter events, 14.9 us)
Async XLA Ops:
  6.5 133.5 %all-gather.4.cloned.1.call-start = ((), (), s32[]{:S(2)}) async-start(), calls=%async_computation | async-start | bytes 3244032 | tf_op jit(solution)/shard_map/gather_inputs/all_gather | solution.py:156
  150.6 1.0 copy-start.3
  150.6 1.4 copy-start.5
  157.6 2.5 %copy-start = (f32[512,512]{1,0:T(8,128)S(1)}, f32[512,512]{1,0:T(8,128)}, u32[]{:S(2)}) copy-start(f32[512,512]{1,0:T(8,128)} %get-tuple-element.73) | copy-start | bytes 3145732
  162.5 55.5 %copy-start.1 = (f32[448,512]{1,0:T(8,128)S(1)}, f32[448,512]{1,0:T(8,128)}, u32[]{:S(2)}) copy-start(f32[448,512]{1,0:T(8,128)} %convolution_subtract_fusion.1) | copy-start | bytes 2752516
  216.5 1.5 copy-start.6
  218.0 2.4 %copy-start.4 = (f32[224,448]{1,0:T(8,128)S(1)}, f32[224,448]{1,0:T(8,128)}, u32[]{:S(2)}) copy-start(f32[224,448]{1,0:T(8,128)} %convolution_subtract_fusion.3) | copy-start | bytes 1204228
  220.4 2.4 copy-start.2
Sparse Core Ops, SparseCore 0:
  47.1 63.7 all-gather.3

commit v6 on v5

--- a/solution.py
+++ b/solution.py
@@ -195,12 +195,20 @@
         second_tile = lax.dynamic_slice(second_factor, (start_row, start_col), (tile_rows, tile_cols))
         first_cols = lax.dynamic_slice_in_dim(first_own, start_col, tile_cols, 1)
         second_cols = lax.dynamic_slice_in_dim(second_own, start_col, tile_cols, 1)
-        result = jnp.zeros((NT * tile_rows, NT * tile_cols), jnp.float32)
-        result = result.at[:tile_rows, :tile_cols].set(first_corner)
-        result = result.at[tile_rows:, :tile_cols].set(first_cols)
-        result = result.at[tile_rows : 2 * tile_rows, tile_cols : 2 * tile_cols].set(second_tile)
-        result = result.at[2 * tile_rows :, tile_cols : 2 * tile_cols].set(second_cols)
-        result = result.at[2 * tile_rows :, 2 * tile_cols :].set(trailing)
+        width = NT * tile_cols
+        first_block = jnp.concatenate(
+            [first_corner, jnp.zeros((tile_rows, width - tile_cols), jnp.float32)], axis=1
+        )
+        second_block = jnp.concatenate(
+            [
+                first_cols[:tile_rows],
+                second_tile,
+                jnp.zeros((tile_rows, width - 2 * tile_cols), jnp.float32),
+            ],
+            axis=1,
+        )
+        rest_block = jnp.concatenate([first_cols[tile_rows:], second_cols, trailing], axis=1)
+        result = jnp.concatenate([first_block, second_block, rest_block], axis=0)
         result = result.reshape(NT, tile_rows, NT, tile_cols).transpose(0, 2, 1, 3)
     return result.reshape(NT, 1, NT, 1, tile_rows * tile_cols)
 

time: 242 us -> 235 us (0.971)
  local copies, waits for them, and re-layouts: 32 us -> 24.6 us
    scatter x5 -> x0, local copies, waits for them, and re-layouts: 7.49 us -> none  [the longest x1 2.13 us: per_device(): result = result.at[2 * tile_rows:, tile_cols:2 * tile_cols].set(second_cols)]
    unnamed x20 -> x18, local copies, waits for them, and re-layouts: 6.71 us -> 6.69 us
  transfers between devices with their start and end apart: 1 -> 1, of which waited for: 0 -> 0; matrix products, arithmetic and copies ran while one was open for 3% -> 2% of each run, Pallas kernels for 22% -> 23%
where the time goes in v6:
time: 235 us
  Pallas kernels  108 us (46%)
  blocking collectives  68.2 us (29%)
  local copies, waits for them, and re-layouts  24.6 us (10%)
  between operations  13.7 us (6%)
  matrix products  12.7 us (5%)
  other arithmetic  7.92 us (3%)
    pallas_call x2, Pallas kernels, factor_and_inverse(): pl.pallas_call(factor_kernel, out_shape=(jax.ShapeDtypeStruct((size, size...  108 us
    all_gather x1, blocking collectives, per_device(): band = lax.all_gather(local[:, :2 * tile_cols], 'col', axis=0)  35.4 us
    all_gather x1, blocking collectives, per_device(): lax.all_gather(band[:tile_rows, :P_SIZE], 'row', axis=0, tiled=True)  32.7 us
    dot_general x2, matrix products, exact_dot(): lax.dot_general(left_side, right_side, (((1,), (1,)), ((), ())), precisio...  8.03 us
    unnamed x18, local copies, waits for them, and re-layouts  6.69 us
  transfers between devices with their start and end apart: 1, of which 0 were waited for; matrix products, arithmetic and copies ran while one was open for 2% of the time, Pallas kernels for 23%

profile of v6, /device:TPU:1, one launch (start us, length us, event | category | flops | bytes accessed | tf_op | source)
XLA Modules:
  0.0 234.8 jit_solution(3080857557307328065)
XLA Ops:
  6.5 1.7 reshape.28
  8.5 1.0 reshape.29
  9.6 35.4 %all-gather = bf16[4096,64]{1,0:T(8,128)(2,1)S(1)} all-gather(bf16[256,64]{1,0:T(8,128)(2,1)S(1)} %slice.98), channel_id=2, replica_groups=mesh['row'=32,'col'=16] {'col'}, dimensions={0}, use_global_device_ids=true | all-gather | bytes 557056 | tf_op jit(solution)/shard_map/gather_inputs/all_gather | solution.py:149
  48.4 32.7 %all_gather.17 = bf16[512,512]{1,0:T(8,128)(2,1)S(1)} all-gather(bf16[16,512]{1,0:T(8,128)(2,1)S(1)} %copy.57), channel_id=1, replica_groups=mesh['row'=32,'col'=16] {'row'}, dimensions={0}, use_global_device_ids=true | all-gather | bytes 540672 | tf_op jit(solution)/shard_map/gather_inputs/all_gather | solution.py:153
  81.6 1.2 fusion.11.sym_ref
  82.7 53.7 %first_panel.1 = (f32[512,512]{1,0:T(8,128)}, f32[512,512]{1,0:T(8,128)}) custom-call(f32[512,512]{1,0:T(8,128)} %fusion.11.sym_ref), custom_call_target="tpu_custom_call" | custom-call | tf_op jit(solution)/shard_map/first_panel/pallas_call | solution.py:119
  136.4 1.0 copy.72
  137.4 1.0 copy.76
  139.2 2.8 %convert_bitcast_fusion = f32[2,32,16,1472]{3,2,0,1:T(8,128)S(1)} fusion(bf16[32,2,16,1472]{3,2,1,0:T(8,128)(2,1)} %bitcast.50), kind=kLoop, calls=%fused_computation | loop fusion | flops 1507328 | bytes 9043968 | tf_op jit(solution)/shard_map/gather_inputs/convert_element_type | solution.py:158
  143.0 1.1 fusion.24
  144.1 1.0 constant_dynamic-slice_fusion.2
  145.1 1.2 copy.73
  146.3 1.8 copy.74
  148.1 1.6 maximum_bitcast_fusion
  151.1 5.7 %fusion.25 = (bf16[1232,512]{1,0:T(8,128)(2,1)S(1)}, f32[1232,512]{1,0:T(8,128)}) fusion(f32[512,512]{1,0:T(8,128)S(1)} %copy-done.4, f32[480,512]{1,0:T(8,128)S(1)} %slice.106, f32[240,512]{1,0:T(8,128)S(1)} %copy-done.2, f32[512,512]{1,0:T(8,128)S(1)} %get-tuple-element.14), kind=kOutput, calls=%fused_computation.43 | convolution fusion | flops 3877429248 | bytes 7356416 | tf_op jit(solution)/shard_map/first_panel/dot_general | solution.py:27
  156.7 1.4 convolution_subtract_fusion.1
  158.1 1.1 convolution_subtract_fusion.3
  160.4 1.2 fusion.10.sym_ref
  161.6 54.0 %second_panel.1 = (f32[512,512]{1,0:T(8,128)}, f32[512,512]{1,0:T(8,128)}) custom-call(f32[512,512]{1,0:T(8,128)} %fusion.10.sym_ref), custom_call_target="tpu_custom_call" | custom-call | tf_op jit(solution)/shard_map/second_panel/pallas_call | solution.py:119
  215.6 1.4 convolution_subtract_fusion.4
  217.1 2.4 %fusion.6 = f32[672,512]{1,0:T(8,128)S(1)} fusion(f32[512,512]{1,0:T(8,128)S(1)} %copy-done.5, f32[448,512]{1,0:T(8,128)S(1)} %copy-done.1, f32[224,512]{1,0:T(8,128)S(1)} %convolution_subtract_fusion.4), kind=kOutput, calls=%fused_computation.8 | convolution fusion | flops 2114273280 | bytes 3801088 | tf_op jit(solution)/shard_map/second_panel/dot_general | solution.py:27
  220.7 1.1 slice.107
  222.8 2.0 copy.70
  224.8 3.1 %reshape.33 = f32[16,1,16,1,512]{4,3,2,1,0:T(1,128)} reshape(f32[16,16,16,32]{3,2,1,0:T(8,128)} %copy.70) | data formatting | bytes 1048576 | tf_op jit(solution)/shard_map/reshape | solution.py:213
  (49 shorter events, 10.5 us)
Async XLA Ops:
  6.5 132.6 %all-gather.4.cloned.1.call-start = ((), (), s32[]{:S(2)}) async-start(), calls=%async_computation | async-start | bytes 3244032 | tf_op jit(solution)/shard_map/gather_inputs/all_gather | solution.py:156
  149.7 1.0 copy-start.2
  149.7 1.4 copy-start.4
  156.7 2.5 %copy-start = (f32[512,512]{1,0:T(8,128)S(1)}, f32[512,512]{1,0:T(8,128)}, u32[]{:S(2)}) copy-start(f32[512,512]{1,0:T(8,128)} %get-tuple-element.13) | copy-start | bytes 3145732
  161.6 55.5 %copy-start.1 = (f32[448,512]{1,0:T(8,128)S(1)}, f32[448,512]{1,0:T(8,128)}, u32[]{:S(2)}) copy-start(f32[448,512]{1,0:T(8,128)} %convolution_subtract_fusion.1) | copy-start | bytes 2752516
  215.6 1.5 copy-start.5
  217.1 2.5 %copy-start.3 = (f32[224,448]{1,0:T(8,128)S(1)}, f32[224,448]{1,0:T(8,128)}, u32[]{:S(2)}) copy-start(f32[224,448]{1,0:T(8,128)} %convolution_subtract_fusion.3) | copy-start | bytes 1204228
Sparse Core Ops, SparseCore 0:
  47.2 63.7 all-gather.3

commit v7 on v6

--- a/solution.py
+++ b/solution.py
@@ -26,6 +26,13 @@
 def exact_dot(left_side, right_side):
     return lax.dot_general(
         left_side, right_side, (((1,), (1,)), ((), ())),
+        precision=EXACT, preferred_element_type=jnp.float32,
+    )
+
+
+def column_dot(columns, right_side):
+    return lax.dot_general(
+        columns, right_side, (((0,), (1,)), ((), ())),
         precision=EXACT, preferred_element_type=jnp.float32,
     )
 
@@ -155,31 +162,28 @@
         top = jnp.concatenate([band[: 2 * tile_rows], local[: 2 * tile_rows, 2 * tile_cols :]], axis=1)
         top = lax.all_gather(top, "row", axis=0)
         top = top.reshape(row_count, 2, tile_rows, top.shape[-1]).transpose(1, 0, 2, 3)
-        top = top.reshape(2 * P_SIZE, top.shape[-1]).astype(jnp.float32)
+        top = top.reshape(2 * P_SIZE, top.shape[-1])
         corners = jnp.stack([top[P_SIZE:, :P_SIZE], top[P_SIZE : 2 * P_SIZE, P_SIZE : 2 * P_SIZE]])
+        corners = corners.astype(jnp.float32)
         own_second = lax.dynamic_slice_in_dim(top, P_SIZE + column_index * tile_cols, tile_cols, 1)
-        col_rows = jnp.concatenate([own_second, top[:, 2 * P_SIZE :]], axis=1).T
+        col_cols = jnp.concatenate([own_second, top[:, 2 * P_SIZE :]], axis=1).astype(jnp.float32)
 
     with jax.named_scope("first_panel"):
         first_factor, first_inverse = factor_and_inverse(0.5 * (corner + corner.T))
         own_count = (NT - 1) * tile_rows
-        col_total = (NT - 1) * tile_cols
-        stacked = jnp.concatenate(
-            [corners[0], own_rows[:, :P_SIZE], col_rows[:, :P_SIZE]], axis=0
-        )
+        stacked = jnp.concatenate([corners[0], own_rows[:, :P_SIZE]], axis=0)
         solved = exact_dot(stacked, first_inverse)
         next_rows = solved[:P_SIZE].astype(jnp.bfloat16)
-        first_own = solved[P_SIZE : P_SIZE + own_count]
-        first_col = solved[P_SIZE + own_count :]
+        first_own = solved[P_SIZE:]
+        first_col = column_dot(col_cols[:P_SIZE], first_inverse)
 
     with jax.named_scope("second_panel"):
         second_corner = corners[1] - bf16_gram(next_rows, next_rows)
         second_factor, second_inverse = factor_and_inverse(0.5 * (second_corner + second_corner.T))
         own_below = own_rows[tile_rows:, P_SIZE:] - bf16_gram(first_own[tile_rows:], next_rows)
-        col_below = col_rows[tile_cols:, P_SIZE:] - bf16_gram(first_col[tile_cols:], next_rows)
-        solved = exact_dot(jnp.concatenate([own_below, col_below], axis=0), second_inverse)
-        second_own = solved[: own_count - tile_rows]
-        second_col = solved[own_count - tile_rows :]
+        col_below = col_cols[P_SIZE:, tile_cols:] - bf16_gram(next_rows, first_col[tile_cols:])
+        second_own = exact_dot(own_below, second_inverse)
+        second_col = column_dot(col_below, second_inverse)
 
     with jax.named_scope("trailing_update"):
         trailing = local[2 * tile_rows :, 2 * tile_cols :]

time: 235 us -> 242 us (1.030)
  matrix products: 12.7 us -> 17.6 us
  local copies, waits for them, and re-layouts: 24.6 us -> 29.2 us
  other arithmetic: 7.92 us -> 4.96 us
    dot_general x0 -> x2, matrix products: none -> 5.77 us  [column_dot(): lax.dot_general(columns, right_side, (((0,), (1,)), ((), ())), precision=...]
    slice x7 -> x5, local copies, waits for them, and re-layouts: 2.72 us -> 4.99 us  [the longest x1 1.15 us: per_device(): first_own = solved[P_SIZE:]]
    unnamed x18 -> x28, local copies, waits for them, and re-layouts: 6.69 us -> 7.89 us
  transfers between devices with their start and end apart: 1 -> 1, of which waited for: 0 -> 0; matrix products, arithmetic and copies ran while one was open for 2% -> 2% of each run, Pallas kernels for 23% -> 22%
where the time goes in v7:
time: 242 us; the launch traced here: 241 us
  Pallas kernels  108 us (45%)
  blocking collectives  68.1 us (28%)
  local copies, waits for them, and re-layouts  29.2 us (12%)
  matrix products  17.6 us (7%)
  between operations  13.7 us (6%)
  other arithmetic  4.96 us (2%)
    pallas_call x2, Pallas kernels, factor_and_inverse(): pl.pallas_call(factor_kernel, out_shape=(jax.ShapeDtypeStruct((size, size...  108 us
    all_gather x1, blocking collectives, per_device(): band = lax.all_gather(local[:, :2 * tile_cols], 'col', axis=0)  35.4 us
    all_gather x1, blocking collectives, per_device(): lax.all_gather(band[:tile_rows, :P_SIZE], 'row', axis=0, tiled=True)  32.7 us
    dot_general x2, matrix products, exact_dot(): lax.dot_general(left_side, right_side, (((1,), (1,)), ((), ())), precisio...  8.19 us
    unnamed x28, local copies, waits for them, and re-layouts  7.89 us
    dot_general x2, matrix products, column_dot(): lax.dot_general(columns, right_side, (((0,), (1,)), ((), ())), precision=...  5.77 us
  transfers between devices with their start and end apart: 1, of which 0 were waited for; matrix products, arithmetic and copies ran while one was open for 2% of the time, Pallas kernels for 22%

profile of v7, /device:TPU:1, one launch (start us, length us, event | category | flops | bytes accessed | tf_op | source)
XLA Modules:
  0.0 241.4 jit_solution(4875525538871503361)
XLA Ops:
  6.5 1.7 reshape.28
  8.5 1.0 reshape.29
  10.2 35.4 %all-gather = bf16[4096,64]{1,0:T(8,128)(2,1)S(1)} all-gather(bf16[256,64]{1,0:T(8,128)(2,1)S(1)} %slice.101), channel_id=2, replica_groups=mesh['row'=32,'col'=16] {'col'}, dimensions={0}, use_global_device_ids=true | all-gather | bytes 557056 | tf_op jit(solution)/shard_map/gather_inputs/all_gather | solution.py:156
  47.9 32.7 %all_gather.17 = bf16[512,512]{1,0:T(8,128)(2,1)S(1)} all-gather(bf16[16,512]{1,0:T(8,128)(2,1)S(1)} %copy.51), channel_id=1, replica_groups=mesh['row'=32,'col'=16] {'row'}, dimensions={0}, use_global_device_ids=true | all-gather | bytes 540672 | tf_op jit(solution)/shard_map/gather_inputs/all_gather | solution.py:160
  83.6 1.2 fusion.5.sym_ref
  84.8 53.9 %first_panel.1 = (f32[512,512]{1,0:T(8,128)}, f32[512,512]{1,0:T(8,128)}) custom-call(f32[512,512]{1,0:T(8,128)} %fusion.5.sym_ref), custom_call_target="tpu_custom_call" | custom-call | tf_op jit(solution)/shard_map/first_panel/pallas_call | solution.py:126
  139.5 2.1 copy.55
  142.4 1.1 slice.116
  143.5 1.1 fusion.17
  144.6 2.1 copy.66
  146.7 2.1 copy.67
  148.8 1.5 maximum_convert_fusion
  150.4 6.3 %fusion.18 = (bf16[752,512]{1,0:T(8,128)(2,1)S(1)}, f32[752,512]{1,0:T(8,128)}) fusion(f32[512,512]{1,0:T(8,128)S(1)} %copy-done.6, f32[240,512]{0,1:T(8,128)S(1)} %copy-done.7, f32[512,512]{0,1:T(8,128)S(1)} %slice_bitcast_fusion.1), kind=kOutput, calls=%fused_computation.39 | convolution fusion | flops 2366357504 | bytes 4898816 | tf_op jit(solution)/shard_map/first_panel/dot_general | solution.py:27
  156.8 1.5 convolution_subtract_fusion
  158.5 1.1 convolution_subtract_fusion.2
  159.8 1.2 copy.68
  161.0 1.1 slice.110
  163.0 2.8 %fusion.6 = bf16[480,512]{1,0:T(8,128)(2,1)S(1)} fusion(f32[512,512]{1,0:T(8,128)} %get-tuple-element.10, bf16[1024,448]{1,0:T(8,128)(2,1)} %slice.116, bf16[1024,32]{1,0:T(8,128)(2,1)S(1)} %constant_dynamic-slice_fusion.1), kind=kOutput, calls=%fused_computation.20 | convolution fusion | flops 1510932480 | bytes 2523136 | tf_op jit(solution)/shard_map/first_panel/dot_general | solution.py:34
  167.4 1.2 fusion.4.sym_ref
  168.6 53.9 %second_panel.1 = (f32[512,512]{1,0:T(8,128)}, f32[512,512]{1,0:T(8,128)}) custom-call(f32[512,512]{1,0:T(8,128)} %fusion.4.sym_ref), custom_call_target="tpu_custom_call" | custom-call | tf_op jit(solution)/shard_map/second_panel/pallas_call | solution.py:126
  222.6 3.0 %convolution_convert_fusion = bf16[448,512]{1,0:T(8,128)(2,1)S(1)} fusion(f32[512,448]{0,1:T(8,128)S(1)} %convolution_subtract_fusion.1, f32[512,512]{1,0:T(8,128)} %get-tuple-element.12), kind=kOutput, calls=%fused_computation.6 | convolution fusion | flops 1409515520 | bytes 2424832 | tf_op jit(solution)/shard_map/second_panel/dot_general | solution.py:34
  225.6 1.8 fusion.19
  229.4 2.0 copy.63
  231.5 3.1 %reshape.35 = f32[16,1,16,1,512]{4,3,2,1,0:T(1,128)} reshape(f32[16,16,16,32]{3,2,1,0:T(8,128)} %copy.63) | data formatting | bytes 1048576 | tf_op jit(solution)/shard_map/reshape | solution.py:217
  (59 shorter events, 12.7 us)
Async XLA Ops:
  6.5 132.9 %all-gather.4.cloned.1.call-start = ((), (), s32[]{:S(2)}) async-start(), calls=%async_computation | async-start | bytes 3244032 | tf_op jit(solution)/shard_map/gather_inputs/all_gather | solution.py:163
  9.5 0.7 copy-start.9
  81.6 1.0 copy-start.3
  148.7 1.5 copy-start.6
  148.8 1.7 copy-start.7
  156.8 2.9 %copy-start = (bf16[752,512]{1,0:T(8,128)(2,1)}, bf16[752,512]{1,0:T(8,128)(2,1)S(1)}, u32[]{:S(2)}) copy-start(bf16[752,512]{1,0:T(8,128)(2,1)S(1)} %get-tuple-element.15) | copy-start | bytes 2310148
  156.8 1.7 copy-start.4
  161.0 4.8 %copy-start.1 = (bf16[752,512]{1,0:T(8,128)(2,1)S(1)}, bf16[752,512]{1,0:T(8,128)(2,1)}, u32[]{:S(2)}) copy-start(bf16[752,512]{1,0:T(8,128)(2,1)} %copy-done) | copy-start | bytes 2310148
  161.0 4.8 %copy-start.10 = (bf16[256,512]{1,0:T(8,128)(2,1)S(1)}, bf16[256,512]{1,0:T(8,128)(2,1)}, u32[]{:S(2)}) copy-start(bf16[256,512]{1,0:T(8,128)(2,1)} %copy-done.9) | copy-start | bytes 786436
  165.9 1.2 copy-start.2
  168.6 56.9 %copy-start.8 = (f32[224,512]{0,1:T(8,128)S(1)}, f32[224,512]{0,1:T(8,128)}, u32[]{:S(2)}) copy-start(f32[224,512]{0,1:T(8,128)} %convolution_subtract_fusion.2) | copy-start | bytes 1376260
  222.6 3.0 %copy-start.5 = (f32[512,512]{1,0:T(8,128)S(1)}, f32[512,512]{1,0:T(8,128)}, u32[]{:S(2)}) copy-start(f32[512,512]{1,0:T(8,128)} %get-tuple-element.12) | copy-start | bytes 3145732
  225.6 3.1 %copy-start.11 = (f32[224,32]{1,0:T(8,128)S(1)}, f32[224,32]{1,0:T(8,128)}, u32[]{:S(2)}) copy-start(f32[224,32]{1,0:T(8,128)} %dynamic-slice.1) | copy-start | bytes 86020
Sparse Core Ops, SparseCore 0:
  47.7 63.8 all-gather.3

commit v8 on v6

--- a/solution.py
+++ b/solution.py
@@ -27,6 +27,13 @@
     return lax.dot_general(
         left_side, right_side, (((1,), (1,)), ((), ())),
         precision=EXACT, preferred_element_type=jnp.float32,
+    )
+
+
+def solve_dot(left_side, right_side):
+    return lax.dot_general(
+        left_side, right_side, (((1,), (1,)), ((), ())),
+        precision=lax.Precision.HIGH, preferred_element_type=jnp.float32,
     )
 
 
@@ -167,7 +174,7 @@
         stacked = jnp.concatenate(
             [corners[0], own_rows[:, :P_SIZE], col_rows[:, :P_SIZE]], axis=0
         )
-        solved = exact_dot(stacked, first_inverse)
+        solved = solve_dot(stacked, first_inverse)
         next_rows = solved[:P_SIZE].astype(jnp.bfloat16)
         first_own = solved[P_SIZE : P_SIZE + own_count]
         first_col = solved[P_SIZE + own_count :]
@@ -177,7 +184,7 @@
         second_factor, second_inverse = factor_and_inverse(0.5 * (second_corner + second_corner.T))
         own_below = own_rows[tile_rows:, P_SIZE:] - bf16_gram(first_own[tile_rows:], next_rows)
         col_below = col_rows[tile_cols:, P_SIZE:] - bf16_gram(first_col[tile_cols:], next_rows)
-        solved = exact_dot(jnp.concatenate([own_below, col_below], axis=0), second_inverse)
+        solved = solve_dot(jnp.concatenate([own_below, col_below], axis=0), second_inverse)
         second_own = solved[: own_count - tile_rows]
         second_col = solved[own_count - tile_rows :]
 

time: 235 us -> 232 us (0.987)
  matrix products: 12.7 us -> 9.68 us
    dot_general x2, matrix products: 8.03 us -> 5 us  [solve_dot(): lax.dot_general(left_side, right_side, (((1,), (1,)), ((), ())), precisio...]
where the time goes in v8:
time: 232 us
  Pallas kernels  108 us (47%)
  blocking collectives  68 us (29%)
  local copies, waits for them, and re-layouts  24.6 us (11%)
  between operations  13.7 us (6%)
  matrix products  9.68 us (4%)
  other arithmetic  7.92 us (3%)
    pallas_call x2, Pallas kernels, factor_and_inverse(): pl.pallas_call(factor_kernel, out_shape=(jax.ShapeDtypeStruct((size, size...  108 us
    all_gather x1, blocking collectives, per_device(): band = lax.all_gather(local[:, :2 * tile_cols], 'col', axis=0)  35.4 us
    all_gather x1, blocking collectives, per_device(): lax.all_gather(band[:tile_rows, :P_SIZE], 'row', axis=0, tiled=True)  32.5 us
    unnamed x18, local copies, waits for them, and re-layouts  6.69 us
    dot_general x2, matrix products, solve_dot(): lax.dot_general(left_side, right_side, (((1,), (1,)), ((), ())), precisio...  5 us
    dot_general x5, matrix products, bf16_gram(): lax.dot_general(left_side.astype(jnp.bfloat16), right_side.astype(jnp.bfl...  4.69 us
  transfers between devices with their start and end apart: 1, of which 0 were waited for; matrix products, arithmetic and copies ran while one was open for 2% of the time, Pallas kernels for 23%

profile of v8, /device:TPU:1, one launch (start us, length us, event | category | flops | bytes accessed | tf_op | source)
XLA Modules:
  0.0 231.7 jit_solution(14515273410451010429)
XLA Ops:
  6.5 1.7 reshape.28
  8.5 1.0 reshape.29
  9.6 35.4 %all-gather = bf16[4096,64]{1,0:T(8,128)(2,1)S(1)} all-gather(bf16[256,64]{1,0:T(8,128)(2,1)S(1)} %slice.98), channel_id=2, replica_groups=mesh['row'=32,'col'=16] {'col'}, dimensions={0}, use_global_device_ids=true | all-gather | bytes 557056 | tf_op jit(solution)/shard_map/gather_inputs/all_gather | solution.py:156
  48.4 32.5 %all_gather.17 = bf16[512,512]{1,0:T(8,128)(2,1)S(1)} all-gather(bf16[16,512]{1,0:T(8,128)(2,1)S(1)} %copy.57), channel_id=1, replica_groups=mesh['row'=32,'col'=16] {'row'}, dimensions={0}, use_global_device_ids=true | all-gather | bytes 540672 | tf_op jit(solution)/shard_map/gather_inputs/all_gather | solution.py:160
  81.4 1.2 fusion.11.sym_ref
  82.5 53.9 %first_panel.1 = (f32[512,512]{1,0:T(8,128)}, f32[512,512]{1,0:T(8,128)}) custom-call(f32[512,512]{1,0:T(8,128)} %fusion.11.sym_ref), custom_call_target="tpu_custom_call" | custom-call | tf_op jit(solution)/shard_map/first_panel/pallas_call | solution.py:126
  136.4 1.0 copy.72
  137.4 1.0 copy.76
  139.2 2.8 %convert_bitcast_fusion = f32[2,32,16,1472]{3,2,0,1:T(8,128)S(1)} fusion(bf16[32,2,16,1472]{3,2,1,0:T(8,128)(2,1)} %bitcast.50), kind=kLoop, calls=%fused_computation | loop fusion | flops 1507328 | bytes 9043968 | tf_op jit(solution)/shard_map/gather_inputs/convert_element_type | solution.py:165
  142.9 1.1 fusion.24
  144.1 1.0 constant_dynamic-slice_fusion.2
  145.1 1.2 copy.73
  146.3 1.8 copy.74
  148.1 1.6 maximum_bitcast_fusion
  151.1 3.7 %fusion.25 = (bf16[1232,512]{1,0:T(8,128)(2,1)S(1)}, f32[1232,512]{1,0:T(8,128)}) fusion(f32[512,512]{1,0:T(8,128)S(1)} %copy-done.4, f32[480,512]{1,0:T(8,128)S(1)} %slice.106, f32[240,512]{1,0:T(8,128)S(1)} %copy-done.2, f32[512,512]{1,0:T(8,128)S(1)} %get-tuple-element.14), kind=kOutput, calls=%fused_computation.43 | convolution fusion | flops 1939660800 | bytes 7356416 | tf_op jit(solution)/shard_map/first_panel/dot_general | solution.py:34
  154.8 1.4 convolution_subtract_fusion.1
  156.1 1.1 convolution_subtract_fusion.3
  158.4 1.2 fusion.10.sym_ref
  159.6 54.0 %second_panel.1 = (f32[512,512]{1,0:T(8,128)}, f32[512,512]{1,0:T(8,128)}) custom-call(f32[512,512]{1,0:T(8,128)} %fusion.10.sym_ref), custom_call_target="tpu_custom_call" | custom-call | tf_op jit(solution)/shard_map/second_panel/pallas_call | solution.py:126
  213.6 1.4 convolution_subtract_fusion.4
  215.1 1.3 fusion.6
  217.7 1.1 slice.107
  219.7 2.0 copy.70
  221.7 3.1 %reshape.33 = f32[16,1,16,1,512]{4,3,2,1,0:T(1,128)} reshape(f32[16,16,16,32]{3,2,1,0:T(8,128)} %copy.70) | data formatting | bytes 1048576 | tf_op jit(solution)/shard_map/reshape | solution.py:220
  (49 shorter events, 10.5 us)
Async XLA Ops:
  6.5 132.6 %all-gather.4.cloned.1.call-start = ((), (), s32[]{:S(2)}) async-start(), calls=%async_computation | async-start | bytes 3244032 | tf_op jit(solution)/shard_map/gather_inputs/all_gather | solution.py:163
  149.7 1.0 copy-start.2
  149.7 1.4 copy-start.4
  154.8 2.5 %copy-start = (f32[512,512]{1,0:T(8,128)S(1)}, f32[512,512]{1,0:T(8,128)}, u32[]{:S(2)}) copy-start(f32[512,512]{1,0:T(8,128)} %get-tuple-element.13) | copy-start | bytes 3145732
  159.6 55.4 %copy-start.1 = (f32[448,512]{1,0:T(8,128)S(1)}, f32[448,512]{1,0:T(8,128)}, u32[]{:S(2)}) copy-start(f32[448,512]{1,0:T(8,128)} %convolution_subtract_fusion.1) | copy-start | bytes 2752516
  213.6 1.5 copy-start.5
  215.1 1.5 copy-start.3
Sparse Core Ops, SparseCore 0:
  47.2 63.7 all-gather.3

commit v9 on v6

--- a/solution.py
+++ b/solution.py
@@ -28,6 +28,18 @@
         left_side, right_side, (((1,), (1,)), ((), ())),
         precision=EXACT, preferred_element_type=jnp.float32,
     )
+
+
+def split_dot(narrow_side, right_side):
+    parts = []
+    remainder = right_side
+    for _ in range(3):
+        piece = lax.reduce_precision(remainder, exponent_bits=8, mantissa_bits=7)
+        parts.append(piece.astype(jnp.bfloat16))
+        remainder = remainder - piece
+    narrow_side = narrow_side.astype(jnp.bfloat16)
+    total = bf16_gram(narrow_side, parts[0])
+    return total + (bf16_gram(narrow_side, parts[1]) + bf16_gram(narrow_side, parts[2]))
 
 
 def factor_kernel(sym_ref, low_ref, inv_ref, work_ref, diag_ref, dinv_ref):
@@ -167,7 +179,7 @@
         stacked = jnp.concatenate(
             [corners[0], own_rows[:, :P_SIZE], col_rows[:, :P_SIZE]], axis=0
         )
-        solved = exact_dot(stacked, first_inverse)
+        solved = split_dot(stacked, first_inverse)
         next_rows = solved[:P_SIZE].astype(jnp.bfloat16)
         first_own = solved[P_SIZE : P_SIZE + own_count]
         first_col = solved[P_SIZE + own_count :]

time: 235 us -> 228 us (0.970)
  other arithmetic: 7.92 us -> 4.07 us
  matrix products: 12.7 us -> 8.96 us
    convert_element_type x1 -> x2, local copies, waits for them, and re-layouts: 0.81 us -> 5.3 us  [per_device(): top = top.reshape(2 * P_SIZE, top.shape[-1]).astype(jnp.float32)]
    dot_general x2 -> x1, matrix products: 8.03 us -> 3.73 us  [exact_dot(): lax.dot_general(left_side, right_side, (((1,), (1,)), ((), ())), precisio...]
    unnamed x18 -> x17, local copies, waits for them, and re-layouts: 6.69 us -> 5.96 us
    dot_general x5 -> x8, matrix products: 4.68 us -> 5.23 us  [bf16_gram(): lax.dot_general(left_side.astype(jnp.bfloat16), right_side.astype(jnp.bfl...]
  transfers between devices with their start and end apart: 1 -> 1, of which waited for: 0 -> 0; matrix products, arithmetic and copies ran while one was open for 2% -> 2% of each run, Pallas kernels for 23% -> 24%
where the time goes in v9:
time: 228 us
  Pallas kernels  108 us (47%)
  blocking collectives  67.9 us (30%)
  local copies, waits for them, and re-layouts  25.6 us (11%)
  between operations  13.7 us (6%)
  matrix products  8.96 us (4%)
  other arithmetic  4.07 us (2%)
    pallas_call x2, Pallas kernels, factor_and_inverse(): pl.pallas_call(factor_kernel, out_shape=(jax.ShapeDtypeStruct((size, size...  108 us
    all_gather x1, blocking collectives, per_device(): band = lax.all_gather(local[:, :2 * tile_cols], 'col', axis=0)  35.4 us
    all_gather x1, blocking collectives, per_device(): lax.all_gather(band[:tile_rows, :P_SIZE], 'row', axis=0, tiled=True)  32.5 us
    unnamed x17, local copies, waits for them, and re-layouts  5.96 us
    convert_element_type x2, local copies, waits for them, and re-layouts, per_device(): top = top.reshape(2 * P_SIZE, top.shape[-1]).astype(jnp.float32)  5.3 us
    dot_general x8, matrix products, bf16_gram(): lax.dot_general(left_side.astype(jnp.bfloat16), right_side.astype(jnp.bfl...  5.23 us
  transfers between devices with their start and end apart: 1, of which 0 were waited for; matrix products, arithmetic and copies ran while one was open for 2% of the time, Pallas kernels for 24%

profile of v9, /device:TPU:1, one launch (start us, length us, event | category | flops | bytes accessed | tf_op | source)
XLA Modules:
  0.0 228.0 jit_solution(303120060921406975)
XLA Ops:
  6.5 1.7 reshape.28
  8.5 1.0 reshape.29
  10.3 35.4 %all-gather = bf16[4096,64]{1,0:T(8,128)(2,1)S(1)} all-gather(bf16[256,64]{1,0:T(8,128)(2,1)S(1)} %slice.105), channel_id=2, replica_groups=mesh['row'=32,'col'=16] {'col'}, dimensions={0}, use_global_device_ids=true | all-gather | bytes 557056 | tf_op jit(solution)/shard_map/gather_inputs/all_gather | solution.py:161
  48.5 0.8 copy.67
  49.3 0.8 copy.66
  50.2 32.5 %all_gather.17 = bf16[512,512]{1,0:T(8,128)(2,1)S(1)} all-gather(bf16[16,512]{1,0:T(8,128)(2,1)S(1)} %copy.53), channel_id=1, replica_groups=mesh['row'=32,'col'=16] {'row'}, dimensions={0}, use_global_device_ids=true | all-gather | bytes 540672 | tf_op jit(solution)/shard_map/gather_inputs/all_gather | solution.py:165
  83.1 1.1 fusion.7.sym_ref
  84.2 53.8 %first_panel.1 = (f32[512,512]{1,0:T(8,128)}, f32[512,512]{1,0:T(8,128)}) custom-call(f32[512,512]{1,0:T(8,128)} %fusion.7.sym_ref), custom_call_target="tpu_custom_call" | custom-call | tf_op jit(solution)/shard_map/first_panel/pallas_call | solution.py:131
  138.1 0.8 dynamic_slice.15
  138.9 2.1 copy.57
  141.0 1.6 copy-done
  142.6 3.2 %copy.60 = bf16[1024,1472]{0,1:T(8,128)(2,1)S(1)} copy(bf16[1024,1472]{1,0:T(8,128)(2,1)} %bitcast.39) | data formatting | bytes 6029312 | tf_op jit(solution)/shard_map/gather_inputs/convert_element_type | solution.py:170
  147.0 1.0 copy-done.1
  148.0 0.9 fusion.9
  148.9 0.9 convolution_add_fusion
  149.8 0.9 fusion.21
  152.5 0.7 dynamic-slice.1
  153.3 1.1 convolution_subtract_fusion.4
  154.7 1.2 fusion.6.sym_ref
  155.9 53.9 %second_panel.1 = (f32[512,512]{1,0:T(8,128)}, f32[512,512]{1,0:T(8,128)}) custom-call(f32[512,512]{1,0:T(8,128)} %fusion.6.sym_ref), custom_call_target="tpu_custom_call" | custom-call | tf_op jit(solution)/shard_map/second_panel/pallas_call | solution.py:131
  209.8 0.8 dynamic_slice.18
  210.6 3.7 %fusion = f32[672,512]{1,0:T(8,128)S(1)} fusion(f32[512,512]{1,0:T(8,128)} %get-tuple-element.12, f32[448,512]{1,0:T(8,128)S(1)} %convolution_subtract_fusion.1, f32[224,512]{1,0:T(8,128)} %convolution_subtract_fusion.4), kind=kOutput, calls=%fused_computation.7 | convolution fusion | flops 2114273280 | bytes 3801088 | tf_op jit(solution)/shard_map/second_panel/dot_general | solution.py:27
  216.0 2.0 copy.64
  218.0 3.1 %reshape.33 = f32[16,1,16,1,512]{4,3,2,1,0:T(1,128)} reshape(f32[16,16,16,32]{3,2,1,0:T(8,128)} %copy.64) | data formatting | bytes 1048576 | tf_op jit(solution)/shard_map/reshape | solution.py:225
  (51 shorter events, 9.1 us)
Async XLA Ops:
  6.5 132.3 %all-gather.4.cloned.1.call-start = ((), (), s32[]{:S(2)}) async-start(), calls=%async_computation | async-start | bytes 3244032 | tf_op jit(solution)/shard_map/gather_inputs/all_gather | solution.py:168
  9.5 0.7 copy-start.3
  141.0 1.6 copy-start
  146.8 1.2 copy-start.1
  146.8 1.3 copy-start.2
  151.1 1.0 copy-start.4
  152.1 1.2 copy-start.5
  214.3 0.9 copy-start.6
Sparse Core Ops, SparseCore 0:
  47.8 63.7 all-gather.3

commit v10 on v9

--- a/solution.py
+++ b/solution.py
@@ -161,13 +161,13 @@
         band = lax.all_gather(local[:, : 2 * tile_cols], "col", axis=0)
         band = band.reshape(col_count, NT * tile_rows, 2, tile_cols)
         band = band.transpose(1, 2, 0, 3).reshape(NT * tile_rows, 2 * P_SIZE)
-        own_rows = band[tile_rows:].astype(jnp.float32)
+        own_rows = band[tile_rows:]
         corner = lax.all_gather(band[:tile_rows, :P_SIZE], "row", axis=0, tiled=True)
         corner = corner.astype(jnp.float32)
         top = jnp.concatenate([band[: 2 * tile_rows], local[: 2 * tile_rows, 2 * tile_cols :]], axis=1)
         top = lax.all_gather(top, "row", axis=0)
         top = top.reshape(row_count, 2, tile_rows, top.shape[-1]).transpose(1, 0, 2, 3)
-        top = top.reshape(2 * P_SIZE, top.shape[-1]).astype(jnp.float32)
+        top = top.reshape(2 * P_SIZE, top.shape[-1])
         corners = jnp.stack([top[P_SIZE:, :P_SIZE], top[P_SIZE : 2 * P_SIZE, P_SIZE : 2 * P_SIZE]])
         own_second = lax.dynamic_slice_in_dim(top, P_SIZE + column_index * tile_cols, tile_cols, 1)
         col_rows = jnp.concatenate([own_second, top[:, 2 * P_SIZE :]], axis=1).T
@@ -185,10 +185,10 @@
         first_col = solved[P_SIZE + own_count :]
 
     with jax.named_scope("second_panel"):
-        second_corner = corners[1] - bf16_gram(next_rows, next_rows)
+        second_corner = corners[1].astype(jnp.float32) - bf16_gram(next_rows, next_rows)
         second_factor, second_inverse = factor_and_inverse(0.5 * (second_corner + second_corner.T))
-        own_below = own_rows[tile_rows:, P_SIZE:] - bf16_gram(first_own[tile_rows:], next_rows)
-        col_below = col_rows[tile_cols:, P_SIZE:] - bf16_gram(first_col[tile_cols:], next_rows)
+        own_below = own_rows[tile_rows:, P_SIZE:].astype(jnp.float32) - bf16_gram(first_own[tile_rows:], next_rows)
+        col_below = col_rows[tile_cols:, P_SIZE:].astype(jnp.float32) - bf16_gram(first_col[tile_cols:], next_rows)
         solved = exact_dot(jnp.concatenate([own_below, col_below], axis=0), second_inverse)
         second_own = solved[: own_count - tile_rows]
         second_col = solved[own_count - tile_rows :]

time: 228 us -> 226 us (level)
  local copies, waits for them, and re-layouts: 25.6 us -> 20.4 us
    convert_element_type x2 -> x0, local copies, waits for them, and re-layouts: 5.3 us -> none  [per_device(): top = top.reshape(2 * P_SIZE, top.shape[-1]).astype(jnp.float32)]
    unnamed x17 -> x16, local copies, waits for them, and re-layouts: 5.96 us -> 3.55 us
where the time goes in v10:
time: 226 us; the launch traced here: 225 us
  Pallas kernels  108 us (48%)
  blocking collectives  68 us (30%)
  local copies, waits for them, and re-layouts  20.4 us (9%)
  between operations  13.7 us (6%)
  matrix products  11.1 us (5%)
  other arithmetic  4.26 us (2%)
    pallas_call x2, Pallas kernels, factor_and_inverse(): pl.pallas_call(factor_kernel, out_shape=(jax.ShapeDtypeStruct((size, size...  108 us
    all_gather x1, blocking collectives, per_device(): band = lax.all_gather(local[:, :2 * tile_cols], 'col', axis=0)  35.4 us
    all_gather x1, blocking collectives, per_device(): lax.all_gather(band[:tile_rows, :P_SIZE], 'row', axis=0, tiled=True)  32.5 us
    dot_general x8, matrix products, bf16_gram(): lax.dot_general(left_side.astype(jnp.bfloat16), right_side.astype(jnp.bfl...  7.47 us
  transfers between devices with their start and end apart: 1, of which 0 were waited for; matrix products, arithmetic and copies ran while one was open for 2% of the time, Pallas kernels for 24%

profile of v10, /device:TPU:1, one launch (start us, length us, event | category | flops | bytes accessed | tf_op | source)
XLA Modules:
  0.0 225.3 jit_solution(13100124435179566569)
XLA Ops:
  6.5 1.7 reshape.26
  8.5 1.0 reshape.27
  9.6 35.4 %all-gather = bf16[4096,64]{1,0:T(8,128)(2,1)S(1)} all-gather(bf16[256,64]{1,0:T(8,128)(2,1)S(1)} %slice.101), channel_id=2, replica_groups=mesh['row'=32,'col'=16] {'col'}, dimensions={0}, use_global_device_ids=true | all-gather | bytes 557056 | tf_op jit(solution)/shard_map/gather_inputs/all_gather | solution.py:161
  47.9 0.8 copy.76
  48.9 32.5 %all_gather.17 = bf16[512,512]{1,0:T(8,128)(2,1)S(1)} all-gather(bf16[16,512]{1,0:T(8,128)(2,1)S(1)} %copy.57), channel_id=1, replica_groups=mesh['row'=32,'col'=16] {'row'}, dimensions={0}, use_global_device_ids=true | all-gather | bytes 540672 | tf_op jit(solution)/shard_map/gather_inputs/all_gather | solution.py:165
  81.8 1.1 fusion.7.sym_ref
  83.0 53.9 %first_panel.1 = (f32[512,512]{1,0:T(8,128)}, f32[512,512]{1,0:T(8,128)}) custom-call(f32[512,512]{1,0:T(8,128)} %fusion.7.sym_ref), custom_call_target="tpu_custom_call" | custom-call | tf_op jit(solution)/shard_map/first_panel/pallas_call | solution.py:131
  136.8 0.8 dynamic_slice.15
  137.6 2.1 copy.61
  140.0 0.8 copy.73
  141.3 1.0 maximum_bitcast_fusion
  142.6 0.9 fusion.9
  143.4 0.9 convolution_add_fusion
  144.3 2.3 %fusion.22 = (bf16[1232,512]{1,0:T(8,128)(2,1)S(1)}, f32[1232,512]{1,0:T(8,128)}) fusion(f32[1232,512]{1,0:T(8,128)S(1)} %convolution_add_fusion, f32[512,512]{1,0:T(8,128)S(1)} %copy-done, bf16[480,512]{1,0:T(8,128)(2,1)S(1)} %slice.109, bf16[240,512]{1,0:T(8,128)(2,1)S(1)} %copy.72, bf16[512,512]{1,0:T(8,128)(2,1)S(1)} %get-tuple-element.14), kind=kOutput, calls=%fused_computation.44 | convolution fusion | flops 651493376 | bytes 8617984 | tf_op jit(solution)/shard_map/first_panel/dot_general | solution.py:13
  147.1 1.1 convolution_subtract_fusion.3
  148.2 1.0 copy.75
  149.2 1.1 slice.110
  150.5 1.1 convolution_subtract_fusion.4
  152.4 1.2 fusion.6.sym_ref
  153.6 53.9 %second_panel.1 = (f32[512,512]{1,0:T(8,128)}, f32[512,512]{1,0:T(8,128)}) custom-call(f32[512,512]{1,0:T(8,128)} %fusion.6.sym_ref), custom_call_target="tpu_custom_call" | custom-call | tf_op jit(solution)/shard_map/second_panel/pallas_call | solution.py:131
  207.6 0.8 dynamic_slice.18
  208.4 3.6 %fusion = f32[672,512]{1,0:T(8,128)S(1)} fusion(f32[512,512]{1,0:T(8,128)} %get-tuple-element.12, f32[448,512]{1,0:T(8,128)S(1)} %convolution_subtract_fusion.1, f32[224,512]{1,0:T(8,128)S(1)} %copy-done.3), kind=kOutput, calls=%fused_computation.6 | convolution fusion | flops 2114273280 | bytes 3801088 | tf_op jit(solution)/shard_map/second_panel/dot_general | solution.py:27
  213.3 2.0 copy.70
  215.3 3.1 %reshape.33 = f32[16,1,16,1,512]{4,3,2,1,0:T(1,128)} reshape(f32[16,16,16,32]{3,2,1,0:T(8,128)} %copy.70) | data formatting | bytes 1048576 | tf_op jit(solution)/shard_map/reshape | solution.py:225
  (48 shorter events, 7.3 us)
Async XLA Ops:
  6.5 131.1 %all-gather.4.cloned.1.call-start = ((), (), s32[]{:S(2)}) async-start(), calls=%async_computation | async-start | bytes 3244032 | tf_op jit(solution)/shard_map/gather_inputs/all_gather | solution.py:168
  141.3 1.3 copy-start
  148.2 2.3 %copy-start.4 = (bf16[224,512]{1,0:T(8,128)(2,1)S(1)}, bf16[224,512]{1,0:T(8,128)(2,1)}, u32[]{:S(2)}) copy-start(bf16[224,512]{1,0:T(8,128)(2,1)} %copy.76) | copy-start | bytes 688132
  149.2 2.4 %copy-start.1 = (bf16[512,512]{0,1:T(8,128)(2,1)S(1)}, bf16[512,512]{0,1:T(8,128)(2,1)}, u32[]{:S(2)}) copy-start(bf16[512,512]{0,1:T(8,128)(2,1)} %copy.75) | copy-start | bytes 1572868
  153.6 54.7 %copy-start.3 = (f32[224,512]{1,0:T(8,128)S(1)}, f32[224,512]{1,0:T(8,128)}, u32[]{:S(2)}) copy-start(f32[224,512]{1,0:T(8,128)} %convolution_subtract_fusion.4) | copy-start | bytes 1376260
  208.3 3.7 %copy-start.2 = (f32[224,448]{1,0:T(8,128)S(1)}, f32[224,448]{1,0:T(8,128)}, u32[]{:S(2)}) copy-start(f32[224,448]{1,0:T(8,128)} %convolution_subtract_fusion.3) | copy-start | bytes 1204228
Sparse Core Ops, SparseCore 0:
  47.2 63.6 all-gather.3

commit v11 on v10

--- a/solution.py
+++ b/solution.py
@@ -37,9 +37,9 @@
         piece = lax.reduce_precision(remainder, exponent_bits=8, mantissa_bits=7)
         parts.append(piece.astype(jnp.bfloat16))
         remainder = remainder - piece
-    narrow_side = narrow_side.astype(jnp.bfloat16)
-    total = bf16_gram(narrow_side, parts[0])
-    return total + (bf16_gram(narrow_side, parts[1]) + bf16_gram(narrow_side, parts[2]))
+    size = right_side.shape[0]
+    wide = bf16_gram(narrow_side.astype(jnp.bfloat16), jnp.concatenate(parts, axis=0))
+    return wide[:, :size] + (wide[:, size : 2 * size] + wide[:, 2 * size :])
 
 
 def factor_kernel(sym_ref, low_ref, inv_ref, work_ref, diag_ref, dinv_ref):

time: 226 us -> 229 us (1.013)
  other arithmetic: 4.26 us -> 8.33 us
    convert_element_type x0 -> x1, other arithmetic: none -> 2.59 us  [split_dot(): parts.append(piece.astype(jnp.bfloat16))]
    another operation x0 -> x1, other arithmetic: none -> 2.42 us
    dot_general x8 -> x6, matrix products: 7.47 us -> 5.59 us  [bf16_gram(): lax.dot_general(left_side.astype(jnp.bfloat16), right_side.astype(jnp.bfl...]
  transfers between devices with their start and end apart: 1 -> 1, of which waited for: 0 -> 0; matrix products, arithmetic and copies ran while one was open for 2% -> 3% of each run, Pallas kernels for 24% -> 24%
where the time goes in v11:
time: 229 us; the launch traced here: 228 us
  Pallas kernels  108 us (47%)
  blocking collectives  68 us (30%)
  local copies, waits for them, and re-layouts  21 us (9%)
  between operations  13.7 us (6%)
  matrix products  9.37 us (4%)
  other arithmetic  8.33 us (4%)
    pallas_call x2, Pallas kernels, factor_and_inverse(): pl.pallas_call(factor_kernel, out_shape=(jax.ShapeDtypeStruct((size, size...  108 us
    all_gather x1, blocking collectives, per_device(): band = lax.all_gather(local[:, :2 * tile_cols], 'col', axis=0)  35.4 us
    all_gather x1, blocking collectives, per_device(): lax.all_gather(band[:tile_rows, :P_SIZE], 'row', axis=0, tiled=True)  32.6 us
    dot_general x6, matrix products, bf16_gram(): lax.dot_general(left_side.astype(jnp.bfloat16), right_side.astype(jnp.bfl...  5.59 us
  transfers between devices with their start and end apart: 1, of which 0 were waited for; matrix products, arithmetic and copies ran while one was open for 3% of the time, Pallas kernels for 24%

profile of v11, /device:TPU:1, one launch (start us, length us, event | category | flops | bytes accessed | tf_op | source)
XLA Modules:
  0.0 228.2 jit_solution(1993594340525111752)
XLA Ops:
  6.5 1.7 reshape.26
  8.5 1.0 reshape.27
  9.6 35.4 %all-gather = bf16[4096,64]{1,0:T(8,128)(2,1)S(1)} all-gather(bf16[256,64]{1,0:T(8,128)(2,1)S(1)} %slice.113), channel_id=2, replica_groups=mesh['row'=32,'col'=16] {'col'}, dimensions={0}, use_global_device_ids=true | all-gather | bytes 557056 | tf_op jit(solution)/shard_map/gather_inputs/all_gather | solution.py:161
  46.4 0.6 pad_maximum_fusion
  48.2 32.6 %all_gather.17 = bf16[512,512]{1,0:T(8,128)(2,1)S(1)} all-gather(bf16[16,512]{1,0:T(8,128)(2,1)S(1)} %copy.57), channel_id=1, replica_groups=mesh['row'=32,'col'=16] {'row'}, dimensions={0}, use_global_device_ids=true | all-gather | bytes 540672 | tf_op jit(solution)/shard_map/gather_inputs/all_gather | solution.py:165
  81.2 1.1 fusion.19.sym_ref
  82.3 53.8 %first_panel.1 = (f32[512,512]{1,0:T(8,128)}, f32[512,512]{1,0:T(8,128)}) custom-call(f32[512,512]{1,0:T(8,128)} %fusion.19.sym_ref), custom_call_target="tpu_custom_call" | custom-call | tf_op jit(solution)/shard_map/first_panel/pallas_call | solution.py:131
  136.2 0.8 dynamic_slice.15
  136.9 2.6 %reduce-precision_convert_fusion.1 = (bf16[512,512]{1,0:T(8,128)(2,1)}, bf16[512,512]{1,0:T(8,128)(2,1)}, bf16[512,512]{1,0:T(8,128)(2,1)}) fusion(f32[512,512]{1,0:T(8,128)} %get-tuple-element.10), kind=kLoop, calls=%fused_computation.11 | loop fusion | flops 2097152 | bytes 2621440 | tf_op jit(solution)/shard_map/first_panel/convert_element_type | solution.py:38
  139.5 2.1 copy.61
  141.7 0.9 fusion.34
  143.5 0.9 copy-done.2
  144.9 2.2 fusion.1
  147.1 2.4 %fusion.32 = (bf16[1232,512]{1,0:T(8,128)(2,1)S(1)}, f32[1232,512]{1,0:T(8,128)}) fusion(f32[1232,1536]{1,0:T(8,128)S(1)} %fusion.1), kind=kLoop, calls=%fused_computation.53 | loop fusion | flops 1892352 | bytes 11354112 | tf_op jit(solution)/shard_map/convert.3
  149.9 1.1 convolution_subtract_fusion.3
  151.0 1.0 copy.75
  152.0 1.1 slice.125
  153.3 1.1 convolution_subtract_fusion.4
  155.3 1.2 fusion.18.sym_ref
  156.5 53.9 %second_panel.1 = (f32[512,512]{1,0:T(8,128)}, f32[512,512]{1,0:T(8,128)}) custom-call(f32[512,512]{1,0:T(8,128)} %fusion.18.sym_ref), custom_call_target="tpu_custom_call" | custom-call | tf_op jit(solution)/shard_map/second_panel/pallas_call | solution.py:131
  210.4 0.8 dynamic_slice.18
  211.1 3.8 %fusion.7 = f32[672,512]{1,0:T(8,128)S(1)} fusion(f32[512,512]{1,0:T(8,128)} %get-tuple-element.12, f32[448,512]{1,0:T(8,128)S(1)} %convolution_subtract_fusion.1, f32[224,512]{1,0:T(8,128)} %convolution_subtract_fusion.4), kind=kOutput, calls=%fused_computation.12 | convolution fusion | flops 2114273280 | bytes 3801088 | tf_op jit(solution)/shard_map/second_panel/dot_general | solution.py:27
  216.2 2.0 copy.70
  218.2 3.1 %reshape.33 = f32[16,1,16,1,512]{4,3,2,1,0:T(1,128)} reshape(f32[16,16,16,32]{3,2,1,0:T(8,128)} %copy.70) | data formatting | bytes 1048576 | tf_op jit(solution)/shard_map/reshape | solution.py:225
  (50 shorter events, 7.2 us)
Async XLA Ops:
  6.5 133.0 %all-gather.4.cloned.1.call-start = ((), (), s32[]{:S(2)}) async-start(), calls=%async_computation | async-start | bytes 3244032 | tf_op jit(solution)/shard_map/gather_inputs/all_gather | solution.py:168
  143.4 1.0 copy-start.2
  143.4 1.2 copy-start.3
  143.4 1.3 copy-start.4
  143.4 1.5 copy-start.5
  152.0 2.4 %copy-start = (bf16[512,512]{0,1:T(8,128)(2,1)S(1)}, bf16[512,512]{0,1:T(8,128)(2,1)}, u32[]{:S(2)}) copy-start(bf16[512,512]{0,1:T(8,128)(2,1)} %copy.75) | copy-start | bytes 1572868
  211.1 3.8 %copy-start.1 = (f32[224,448]{1,0:T(8,128)S(1)}, f32[224,448]{1,0:T(8,128)}, u32[]{:S(2)}) copy-start(f32[224,448]{1,0:T(8,128)} %convolution_subtract_fusion.3) | copy-start | bytes 1204228
Sparse Core Ops, SparseCore 0:
  47.2 63.7 all-gather.3

commit v12 on v10

--- a/solution.py
+++ b/solution.py
@@ -46,8 +46,11 @@
     size = sym_ref.shape[0]
     blocks = size // BLOCK
     work_ref[...] = sym_ref[...]
-    low_ref[...] = jnp.zeros_like(low_ref)
-    inv_ref[...] = jnp.zeros_like(inv_ref)
+    for i in range(blocks):
+        for k in range(i + 1, blocks):
+            upper = (pl.ds(i * BLOCK, BLOCK), pl.ds(k * BLOCK, BLOCK))
+            low_ref[upper] = jnp.zeros((BLOCK, BLOCK), jnp.float32)
+            inv_ref[upper] = jnp.zeros((BLOCK, BLOCK), jnp.float32)
     rows = lax.broadcasted_iota(jnp.int32, (BLOCK, BLOCK), 0)
     lanes = lax.broadcasted_iota(jnp.int32, (BLOCK, BLOCK), 1)
     col_ids = lax.broadcasted_iota(jnp.int32, (BLOCK, 1), 0)

time: 226 us -> 226 us (level)
  no operation moved by 1% of the time
where the time goes in v12:
time: 226 us; the launch traced here: 225 us
  Pallas kernels  108 us (48%)
  blocking collectives  68 us (30%)
  local copies, waits for them, and re-layouts  20.4 us (9%)
  between operations  13.7 us (6%)
  matrix products  11.1 us (5%)
  other arithmetic  4.26 us (2%)
    pallas_call x2, Pallas kernels, factor_and_inverse(): pl.pallas_call(factor_kernel, out_shape=(jax.ShapeDtypeStruct((size, size...  108 us
    all_gather x1, blocking collectives, per_device(): band = lax.all_gather(local[:, :2 * tile_cols], 'col', axis=0)  35.4 us
    all_gather x1, blocking collectives, per_device(): lax.all_gather(band[:tile_rows, :P_SIZE], 'row', axis=0, tiled=True)  32.5 us
    dot_general x8, matrix products, bf16_gram(): lax.dot_general(left_side.astype(jnp.bfloat16), right_side.astype(jnp.bfl...  7.47 us
  transfers between devices with their start and end apart: 1, of which 0 were waited for; matrix products, arithmetic and copies ran while one was open for 2% of the time, Pallas kernels for 24%

profile of v12, /device:TPU:1, one launch (start us, length us, event | category | flops | bytes accessed | tf_op | source)
XLA Modules:
  0.0 225.2 jit_solution(204849956349175771)
XLA Ops:
  6.5 1.7 reshape.26
  8.5 1.0 reshape.27
  9.6 35.4 %all-gather = bf16[4096,64]{1,0:T(8,128)(2,1)S(1)} all-gather(bf16[256,64]{1,0:T(8,128)(2,1)S(1)} %slice.101), channel_id=2, replica_groups=mesh['row'=32,'col'=16] {'col'}, dimensions={0}, use_global_device_ids=true | all-gather | bytes 557056 | tf_op jit(solution)/shard_map/gather_inputs/all_gather | solution.py:164
  47.9 0.8 copy.76
  48.9 32.5 %all_gather.17 = bf16[512,512]{1,0:T(8,128)(2,1)S(1)} all-gather(bf16[16,512]{1,0:T(8,128)(2,1)S(1)} %copy.57), channel_id=1, replica_groups=mesh['row'=32,'col'=16] {'row'}, dimensions={0}, use_global_device_ids=true | all-gather | bytes 540672 | tf_op jit(solution)/shard_map/gather_inputs/all_gather | solution.py:168
  81.8 1.1 fusion.7.sym_ref
  83.0 53.8 %first_panel.1 = (f32[512,512]{1,0:T(8,128)}, f32[512,512]{1,0:T(8,128)}) custom-call(f32[512,512]{1,0:T(8,128)} %fusion.7.sym_ref), custom_call_target="tpu_custom_call" | custom-call | tf_op jit(solution)/shard_map/first_panel/pallas_call | solution.py:134
  136.8 0.8 dynamic_slice.15
  137.5 2.1 copy.61
  140.0 0.8 copy.73
  141.3 1.0 maximum_bitcast_fusion
  142.5 0.9 fusion.9
  143.4 0.9 convolution_add_fusion
  144.2 2.3 %fusion.22 = (bf16[1232,512]{1,0:T(8,128)(2,1)S(1)}, f32[1232,512]{1,0:T(8,128)}) fusion(f32[1232,512]{1,0:T(8,128)S(1)} %convolution_add_fusion, f32[512,512]{1,0:T(8,128)S(1)} %copy-done, bf16[480,512]{1,0:T(8,128)(2,1)S(1)} %slice.109, bf16[240,512]{1,0:T(8,128)(2,1)S(1)} %copy.72, bf16[512,512]{1,0:T(8,128)(2,1)S(1)} %get-tuple-element.14), kind=kOutput, calls=%fused_computation.44 | convolution fusion | flops 651493376 | bytes 8617984 | tf_op jit(solution)/shard_map/first_panel/dot_general | solution.py:13
  147.0 1.1 convolution_subtract_fusion.3
  148.1 1.0 copy.75
  149.1 1.1 slice.110
  150.4 1.1 convolution_subtract_fusion.4
  152.4 1.2 fusion.6.sym_ref
  153.6 53.9 %second_panel.1 = (f32[512,512]{1,0:T(8,128)}, f32[512,512]{1,0:T(8,128)}) custom-call(f32[512,512]{1,0:T(8,128)} %fusion.6.sym_ref), custom_call_target="tpu_custom_call" | custom-call | tf_op jit(solution)/shard_map/second_panel/pallas_call | solution.py:134
  207.5 0.8 dynamic_slice.18
  208.2 3.6 %fusion = f32[672,512]{1,0:T(8,128)S(1)} fusion(f32[512,512]{1,0:T(8,128)} %get-tuple-element.12, f32[448,512]{1,0:T(8,128)S(1)} %convolution_subtract_fusion.1, f32[224,512]{1,0:T(8,128)S(1)} %copy-done.3), kind=kOutput, calls=%fused_computation.6 | convolution fusion | flops 2114273280 | bytes 3801088 | tf_op jit(solution)/shard_map/second_panel/dot_general | solution.py:27
  213.2 2.0 copy.70
  215.2 3.1 %reshape.33 = f32[16,1,16,1,512]{4,3,2,1,0:T(1,128)} reshape(f32[16,16,16,32]{3,2,1,0:T(8,128)} %copy.70) | data formatting | bytes 1048576 | tf_op jit(solution)/shard_map/reshape | solution.py:228
  (48 shorter events, 7.3 us)
Async XLA Ops:
  6.5 131.0 %all-gather.4.cloned.1.call-start = ((), (), s32[]{:S(2)}) async-start(), calls=%async_computation | async-start | bytes 3244032 | tf_op jit(solution)/shard_map/gather_inputs/all_gather | solution.py:171
  141.2 1.3 copy-start
  148.1 2.3 %copy-start.4 = (bf16[224,512]{1,0:T(8,128)(2,1)S(1)}, bf16[224,512]{1,0:T(8,128)(2,1)}, u32[]{:S(2)}) copy-start(bf16[224,512]{1,0:T(8,128)(2,1)} %copy.76) | copy-start | bytes 688132
  149.1 2.4 %copy-start.1 = (bf16[512,512]{0,1:T(8,128)(2,1)S(1)}, bf16[512,512]{0,1:T(8,128)(2,1)}, u32[]{:S(2)}) copy-start(bf16[512,512]{0,1:T(8,128)(2,1)} %copy.75) | copy-start | bytes 1572868
  153.6 54.7 %copy-start.3 = (f32[224,512]{1,0:T(8,128)S(1)}, f32[224,512]{1,0:T(8,128)}, u32[]{:S(2)}) copy-start(f32[224,512]{1,0:T(8,128)} %convolution_subtract_fusion.4) | copy-start | bytes 1376260
  208.2 3.7 %copy-start.2 = (f32[224,448]{1,0:T(8,128)S(1)}, f32[224,448]{1,0:T(8,128)}, u32[]{:S(2)}) copy-start(f32[224,448]{1,0:T(8,128)} %convolution_subtract_fusion.3) | copy-start | bytes 1204228
Sparse Core Ops, SparseCore 0:
  47.2 63.8 all-gather.3

commit v13 on v10

--- a/solution.py
+++ b/solution.py
@@ -101,7 +101,7 @@
             dinv_ref[...] = inverse
             return block
 
-        lax.fori_loop(0, BLOCK // group, step, work_ref[here, here], unroll=1)
+        lax.fori_loop(0, BLOCK // group, step, work_ref[here, here], unroll=2)
         low_ref[here, here] = diag_ref[...]
         inv_ref[here, here] = dinv_ref[...]
         if k + 1 < blocks:

time: 226 us -> 226 us (level)
  no operation moved by 1% of the time
where the time goes in v13:
time: 226 us; the launch traced here: 225 us
  Pallas kernels  108 us (48%)
  blocking collectives  68 us (30%)
  local copies, waits for them, and re-layouts  20.4 us (9%)
  between operations  13.7 us (6%)
  matrix products  11.1 us (5%)
  other arithmetic  4.26 us (2%)
    pallas_call x2, Pallas kernels, factor_and_inverse(): pl.pallas_call(factor_kernel, out_shape=(jax.ShapeDtypeStruct((size, size...  108 us
    all_gather x1, blocking collectives, per_device(): band = lax.all_gather(local[:, :2 * tile_cols], 'col', axis=0)  35.4 us
    all_gather x1, blocking collectives, per_device(): lax.all_gather(band[:tile_rows, :P_SIZE], 'row', axis=0, tiled=True)  32.5 us
    dot_general x8, matrix products, bf16_gram(): lax.dot_general(left_side.astype(jnp.bfloat16), right_side.astype(jnp.bfl...  7.48 us
  transfers between devices with their start and end apart: 1, of which 0 were waited for; matrix products, arithmetic and copies ran while one was open for 2% of the time, Pallas kernels for 24%

profile of v13, /device:TPU:1, one launch (start us, length us, event | category | flops | bytes accessed | tf_op | source)
XLA Modules:
  0.0 225.4 jit_solution(9658266337518821704)
XLA Ops:
  6.5 1.7 reshape.26
  8.5 1.0 reshape.27
  9.6 35.4 %all-gather = bf16[4096,64]{1,0:T(8,128)(2,1)S(1)} all-gather(bf16[256,64]{1,0:T(8,128)(2,1)S(1)} %slice.101), channel_id=2, replica_groups=mesh['row'=32,'col'=16] {'col'}, dimensions={0}, use_global_device_ids=true | all-gather | bytes 557056 | tf_op jit(solution)/shard_map/gather_inputs/all_gather | solution.py:161
  47.9 0.8 copy.76
  48.9 32.5 %all_gather.17 = bf16[512,512]{1,0:T(8,128)(2,1)S(1)} all-gather(bf16[16,512]{1,0:T(8,128)(2,1)S(1)} %copy.57), channel_id=1, replica_groups=mesh['row'=32,'col'=16] {'row'}, dimensions={0}, use_global_device_ids=true | all-gather | bytes 540672 | tf_op jit(solution)/shard_map/gather_inputs/all_gather | solution.py:165
  81.8 1.1 fusion.7.sym_ref
  83.0 53.9 %first_panel.1 = (f32[512,512]{1,0:T(8,128)}, f32[512,512]{1,0:T(8,128)}) custom-call(f32[512,512]{1,0:T(8,128)} %fusion.7.sym_ref), custom_call_target="tpu_custom_call" | custom-call | tf_op jit(solution)/shard_map/first_panel/pallas_call | solution.py:131
  136.9 0.8 dynamic_slice.15
  137.6 2.1 copy.61
  140.1 0.8 copy.73
  141.4 1.0 maximum_bitcast_fusion
  142.6 0.9 fusion.9
  143.5 0.9 convolution_add_fusion
  144.3 2.3 %fusion.22 = (bf16[1232,512]{1,0:T(8,128)(2,1)S(1)}, f32[1232,512]{1,0:T(8,128)}) fusion(f32[1232,512]{1,0:T(8,128)S(1)} %convolution_add_fusion, f32[512,512]{1,0:T(8,128)S(1)} %copy-done, bf16[480,512]{1,0:T(8,128)(2,1)S(1)} %slice.109, bf16[240,512]{1,0:T(8,128)(2,1)S(1)} %copy.72, bf16[512,512]{1,0:T(8,128)(2,1)S(1)} %get-tuple-element.14), kind=kOutput, calls=%fused_computation.44 | convolution fusion | flops 651493376 | bytes 8617984 | tf_op jit(solution)/shard_map/first_panel/dot_general | solution.py:13
  147.1 1.1 convolution_subtract_fusion.3
  148.2 1.0 copy.75
  149.2 1.1 slice.110
  150.5 1.1 convolution_subtract_fusion.4
  152.5 1.2 fusion.6.sym_ref
  153.7 54.0 %second_panel.1 = (f32[512,512]{1,0:T(8,128)}, f32[512,512]{1,0:T(8,128)}) custom-call(f32[512,512]{1,0:T(8,128)} %fusion.6.sym_ref), custom_call_target="tpu_custom_call" | custom-call | tf_op jit(solution)/shard_map/second_panel/pallas_call | solution.py:131
  207.7 0.8 dynamic_slice.18
  208.5 3.6 %fusion = f32[672,512]{1,0:T(8,128)S(1)} fusion(f32[512,512]{1,0:T(8,128)} %get-tuple-element.12, f32[448,512]{1,0:T(8,128)S(1)} %convolution_subtract_fusion.1, f32[224,512]{1,0:T(8,128)S(1)} %copy-done.3), kind=kOutput, calls=%fused_computation.6 | convolution fusion | flops 2114273280 | bytes 3801088 | tf_op jit(solution)/shard_map/second_panel/dot_general | solution.py:27
  213.4 2.0 copy.70
  215.4 3.1 %reshape.33 = f32[16,1,16,1,512]{4,3,2,1,0:T(1,128)} reshape(f32[16,16,16,32]{3,2,1,0:T(8,128)} %copy.70) | data formatting | bytes 1048576 | tf_op jit(solution)/shard_map/reshape | solution.py:225
  (48 shorter events, 7.4 us)
Async XLA Ops:
  6.5 131.1 %all-gather.4.cloned.1.call-start = ((), (), s32[]{:S(2)}) async-start(), calls=%async_computation | async-start | bytes 3244032 | tf_op jit(solution)/shard_map/gather_inputs/all_gather | solution.py:168
  141.3 1.3 copy-start
  148.2 2.3 %copy-start.4 = (bf16[224,512]{1,0:T(8,128)(2,1)S(1)}, bf16[224,512]{1,0:T(8,128)(2,1)}, u32[]{:S(2)}) copy-start(bf16[224,512]{1,0:T(8,128)(2,1)} %copy.76) | copy-start | bytes 688132
  149.2 2.4 %copy-start.1 = (bf16[512,512]{0,1:T(8,128)(2,1)S(1)}, bf16[512,512]{0,1:T(8,128)(2,1)}, u32[]{:S(2)}) copy-start(bf16[512,512]{0,1:T(8,128)(2,1)} %copy.75) | copy-start | bytes 1572868
  153.7 54.8 %copy-start.3 = (f32[224,512]{1,0:T(8,128)S(1)}, f32[224,512]{1,0:T(8,128)}, u32[]{:S(2)}) copy-start(f32[224,512]{1,0:T(8,128)} %convolution_subtract_fusion.4) | copy-start | bytes 1376260
  208.5 3.7 %copy-start.2 = (f32[224,448]{1,0:T(8,128)S(1)}, f32[224,448]{1,0:T(8,128)}, u32[]{:S(2)}) copy-start(f32[224,448]{1,0:T(8,128)} %convolution_subtract_fusion.3) | copy-start | bytes 1204228
Sparse Core Ops, SparseCore 0:
  47.2 63.8 all-gather.3
